TPU v7x, 32 devices: a whole 2x2x4 slice. The times are simulated.
32 devices in a mesh: lat: 4 (over z), lon: 8 (over y, x, core).
Axes of the slice: x: 2, y: 2, z: 4, core: 2. Of those that a mesh axis runs over, the one named last changes fastest.
Arguments:
- latents: bfloat16 [64, 128, 256], P('lat', 'lon'), may hold values from -6 to 6
- conv_weight: bfloat16 [9, 256, 256], replicated, may hold values from -0.125 to 0.125
- map_weight: bfloat16 [256, 1024], replicated, may hold values from -0.375 to 0.375
- map_bias: float32 [1024], replicated, may hold values from -6 to 6
- input_weight: float32 [3, 512], replicated, may hold values from -3.5 to 3.5
- hidden_weight: bfloat16 [1, 512, 512], replicated, may hold values from -0.25 to 0.25
- output_weight: float32 [512], replicated, may hold values from -0.25 to 0.25
- hit_owner: int32 [768], P(('lat', 'lon')), may hold values from 0 to 31, as said below
- serve_block: int32 [32, 32], P(('lat', 'lon')), may hold values from -1 to 1, as said below
- query_grid: int32 [3, 49152], P(None, ('lat', 'lon')), may hold values from 0 to 127, as said below
- cotangent: float32 [49152], P(('lat', 'lon')), may hold values from -6 to 6
Outputs:
- latent_grad: float32 [64, 128, 256], P('lat', 'lon')
- conv_grad: float32 [9, 256, 256], replicated
- map_grad: float32 [256, 1024], replicated
- map_bias_grad: float32 [1024], replicated
- input_grad: float32 [3, 512], replicated
- hidden_grad: float32 [1, 512, 512], replicated
- output_grad: float32 [512], replicated
Inputs may be any that keep to these rules, and one draw needn't show every extreme that they name: `hit_owner`: each device's 24 entries name distinct devices, numbered lat index times the size of lon plus lon index. `serve_block`: entry [o, r] is a block of device o, 0 to 1, when the list of device r names o, and -1 otherwise. `query_grid`: row 0 is the cell within the block (row-major over 8 rows of 16 cells), row 1 the sub-cell (0 to 35, row-major), row 2 the level (0 to 36).
All inputs are finite; a program needn't handle non-finite values.
Results may differ from a plain program's by a relative error of at most 0.0095.
Values may be sent and summed in bfloat16 or wider, within the bound.
No kernel may reach another device: no remote copies, remote signals or barrier semaphores. Data moves between devices by JAX's collectives and lax.ppermute only.
A program may use at most 128 MiB of HBM per device.

v0:
```python
import functools

import jax
import jax.numpy as jnp
from jax import lax
from jax.experimental import pallas as pl
from jax.experimental.pallas import tpu as pltpu
from jax.sharding import PartitionSpec as P

BLOCK = 128
LEVELS = 37
SUB = 6


OMEGA = 30.0
TILE = 2048
SPAN = 256
PARTS = 8


def conv_apply(padded, kernel, row_count, col_count, flipped):
    channels = padded.shape[-1]
    result = jnp.zeros((row_count * col_count, kernel.shape[-1]), jnp.float32)
    for shift_a in (-1, 0, 1):
        for shift_b in (-1, 0, 1):
            tap_index = (shift_a + 1) * 3 + shift_b + 1
            if flipped:
                window = padded[
                    1 - shift_a : 1 - shift_a + row_count, 1 - shift_b : 1 - shift_b + col_count
                ]
                matrix = kernel[tap_index].T
            else:
                window = padded[
                    1 + shift_a : 1 + shift_a + row_count, 1 + shift_b : 1 + shift_b + col_count
                ]
                matrix = kernel[tap_index]
            result = result + jnp.dot(
                window.reshape(row_count * col_count, channels),
                matrix,
                preferred_element_type=jnp.float32,
            )
    return result


def close_poles(padded, lat_pos, lat_parts):
    top_rim = jnp.where(lat_pos == 0, jnp.zeros_like(padded[:1]), padded[:1])
    bottom_rim = jnp.where(lat_pos == lat_parts - 1, jnp.zeros_like(padded[-1:]), padded[-1:])
    return jnp.concatenate([top_rim, padded[1:-1], bottom_rim], axis=0)


SIN_TERMS = (
    0.7071067781421408,
    -0.029462767114633488,
    0.0003682722504284759,
    -2.1886040931894034e-06,
    7.195418014521965e-09,
)
COS_TERMS = (
    1.4142134959273227,
    -0.17677635831469551,
    0.0036825740917005817,
    -3.061241565438332e-05,
    1.2789559619534725e-07,
)
TURN = 6.283185307179586
TURN_HIGH = 6.28125
TURN_LOW = TURN - TURN_HIGH
EXTRA = 16
COORD_ROWS = 32
CHUNK = 64
LANES = 128


def sin_cos(angle):
    turns = jnp.round(angle * (1.0 / TURN))
    rest = (angle - turns * TURN_HIGH) - turns * TURN_LOW
    square = rest * rest

    def series(terms):
        value = jnp.full_like(square, terms[-1])
        for term in terms[-2::-1]:
            value = value * square + term
        return value

    half_sin = rest * series(SIN_TERMS)
    half_cos = series(COS_TERMS)
    return half_sin * half_cos, 1.0 - half_sin * half_sin


def pack_kernel(
    owner_ref, grid_ref, cotan_ref, tile_ref, sent_ref, first_row, last_row, first_col, last_col
):
    lat_tile, lon_tile, channels = tile_ref.shape
    first_row[...] = tile_ref[:1]
    last_row[...] = tile_ref[lat_tile - 1 :]
    cells = tile_ref[...].reshape(lat_tile * lon_tile, channels).astype(jnp.float32)
    for column, out_ref in ((0, first_col), (lon_tile - 1, last_col)):
        picked = [
            cells[row * lon_tile + column : row * lon_tile + column + 1]
            for row in range(lat_tile)
        ]
        out_ref[...] = jnp.concatenate(picked, axis=0).astype(out_ref.dtype)
    half = LANES // 2
    lower = lax.broadcasted_iota(jnp.int32, (1, LANES), 1) < half
    sent_ref[...] = jnp.zeros_like(sent_ref)
    for pair in range(owner_ref.shape[0] // 2):
        lanes = slice(pair * LANES, (pair + 1) * LANES)
        grid = grid_ref[:, lanes].astype(jnp.float32)
        values = [grid[0:1], grid[1:2], grid[2:3], cotan_ref[lanes].reshape(1, LANES)]
        turned = [pltpu.roll(value, half, 1) for value in values]
        sent_ref[owner_ref[2 * pair]] = jnp.concatenate(
            [
                jnp.where(lower, values[0], turned[1]),
                jnp.where(lower, values[2], turned[3]),
            ],
            axis=1,
        )
        sent_ref[owner_ref[2 * pair + 1]] = jnp.concatenate(
            [
                jnp.where(lower, turned[0], values[1]),
                jnp.where(lower, turned[2], values[3]),
            ],
            axis=1,
        )


def packed(hit_owner, query_grid, cotangent, latents, slots, group_size):
    lat_tile, lon_tile, channels = latents.shape
    row = jax.ShapeDtypeStruct((1, lon_tile, channels), latents.dtype)
    column = jax.ShapeDtypeStruct((lat_tile, channels), latents.dtype)
    vmem = pl.BlockSpec(memory_space=pltpu.VMEM)
    return pl.pallas_call(
        pack_kernel,
        in_specs=[pl.BlockSpec(memory_space=pltpu.SMEM), vmem, vmem, vmem],
        out_specs=[vmem] * 5,
        out_shape=[
            jax.ShapeDtypeStruct((slots, 1, 4 * group_size), jnp.float32),
            row,
            row,
            column,
            column,
        ],
        name="pack",
    )(hit_owner, query_grid, cotangent, latents)


def fetched(sources, targets, sems):
    copies = [
        pltpu.make_async_copy(source, target, sems.at[index])
        for index, (source, target) in enumerate(zip(sources, targets))
    ]
    for copy in copies:
        copy.start()
    return copies


def weights_kernel(cuts, tile_shape, *refs):
    sources, (weight0, weight1, column_tiles), (*targets, sems) = refs[:5], refs[5:8], refs[8:]
    map_ref, bias_ref, input_ref, hidden_ref, output_ref = targets
    for copy in fetched(sources, targets, sems):
        copy.wait()
    channels = map_ref.shape[0]
    hidden = hidden_ref.shape[0]
    f32, bf16 = jnp.float32, jnp.bfloat16
    lat_cell, lat_sub, lon_cell, lon_sub, level_cut, level_offset = cuts
    lat_offset, lon_offset = tile_offsets(tile_shape, cuts)
    weight0[:, :channels] = map_ref[:, :hidden].T
    bias = bias_ref[...].reshape(1, 2 * hidden)
    lat_weight = OMEGA * input_ref[0:1, :]
    lon_weight = OMEGA * input_ref[1:2, :]
    level_weight = OMEGA * input_ref[2:3, :]
    constant = (
        lat_offset * lat_weight
        + lon_offset * lon_weight
        + level_offset * level_weight
        + bias[:, :hidden]
    )
    zero = jnp.zeros_like(constant)
    coef = jnp.concatenate(
        [
            lat_cell * lat_weight,
            lat_sub * lat_weight,
            lon_cell * lon_weight,
            lon_sub * lon_weight,
            level_cut * level_weight,
            constant,
            zero,
            zero,
        ],
        axis=0,
    )
    high = coef.astype(bf16).astype(f32)
    mid = (coef - high).astype(bf16).astype(f32)
    low = coef - high - mid
    parts = jnp.concatenate([high, mid, low, jnp.zeros((LANES - 24, hidden), f32)], axis=0)
    weight0[:, channels:] = parts.T.astype(bf16)
    weight1[:, :hidden] = hidden_ref[...].T
    weight1[:, hidden:] = map_ref[:, hidden:].T
    column_tiles[:, :LANES] = jnp.broadcast_to(bias[:, hidden:], (LANES, hidden)).T
    column_tiles[:, LANES:] = jnp.broadcast_to(
        output_ref[...].reshape(1, hidden), (LANES, hidden)
    ).T


def tile_offsets(tile_shape, cuts):
    lat_step, lon_step = cuts[1], cuts[3]
    lat_base = 2 * SUB * tile_shape[0] * lax.axis_index("lat") + 1
    lon_base = 2 * SUB * tile_shape[1] * lax.axis_index("lon") + 1
    return (
        lat_base.astype(jnp.float32) * (0.5 * lat_step) - 1.0,
        lon_base.astype(jnp.float32) * (0.5 * lon_step) - 1.0,
    )


def prepared_weights(
    tile_shape, map_weight, map_bias, input_weight, hidden_weight, output_weight, cuts
):
    channels = map_weight.shape[0]
    hidden = hidden_weight.shape[0]
    sources = (map_weight, map_bias, input_weight, hidden_weight, output_weight)
    vmem = pl.BlockSpec(memory_space=pltpu.VMEM)
    return pl.pallas_call(
        functools.partial(weights_kernel, cuts, tile_shape),
        in_specs=[pl.BlockSpec(memory_space=pltpu.HBM)] * 5,
        out_specs=[vmem] * 3,
        out_shape=[
            jax.ShapeDtypeStruct((hidden, channels + LANES), jnp.bfloat16),
            jax.ShapeDtypeStruct((hidden, hidden + channels), jnp.bfloat16),
            jax.ShapeDtypeStruct((hidden, 2 * LANES), jnp.float32),
        ],
        scratch_shapes=[pltpu.VMEM(value.shape, value.dtype) for value in sources]
        + [pltpu.SemaphoreType.DMA((5,))],
        name="weights",
    )(*sources)


def query_kernel(
    cuts,
    scale,
    taps,
    single,
    serve_hbm,
    got_ref,
    tile_hbm,
    top_ref,
    bottom_ref,
    left_ref,
    right_ref,
    conv_hbm,
    map_hbm,
    hidden_hbm,
    weight0_hbm,
    weight1_hbm,
    columns_hbm,
    kept_ref,
    away_ref,
    conv_kept_ref,
    conv_away_ref,
    feature_grad_ref,
    serve_ref,
    tile_ref,
    conv_ref,
    map_ref,
    hidden_ref,
    weight0,
    weight1,
    column_tiles,
    sems,
    windows,
    turned,
    shifted,
    fields,
    feat_t,
    stack0,
    lefts,
    pre0,
    pre1,
    cos0,
    rounded0,
    rounded1,
    sums,
    later_sums,
    out_sums,
):
    step = pl.program_id(0)
    lat_tile, lon_tile, channels = tile_ref.shape
    cells = lat_tile * lon_tile
    hidden = hidden_ref.shape[0]
    block = rounded0.shape[1]
    left_rows = cells + EXTRA
    f32, bf16 = jnp.float32, jnp.bfloat16
    lat_cell, lat_sub, lon_cell, lon_sub, level_cut, level_offset = cuts
    lat_pos = lax.axis_index("lat")
    bit = lax.axis_index("lon") & 1
    lat_offset, lon_offset = tile_offsets((lat_tile, lon_tile), cuts)

    @pl.when(step == 0)
    def _():
        copies = fetched(
            (
                tile_hbm,
                serve_hbm,
                conv_hbm,
                weight0_hbm,
                weight1_hbm,
                columns_hbm,
                hidden_hbm,
                map_hbm,
            ),
            (
                tile_ref,
                serve_ref,
                conv_ref,
                weight0,
                weight1,
                column_tiles,
                hidden_ref,
                map_ref,
            ),
            sems,
        )
        copies[1].wait()
        half = LANES // 2
        lower = lax.broadcasted_iota(jnp.int32, (1, LANES), 1) < half
        for pair in range(got_ref.shape[0] // 2):
            even, odd = got_ref[2 * pair], got_ref[2 * pair + 1]
            row = slice(pair, pair + 1)
            for place in range(2):
                lanes = slice(place * LANES, (place + 1) * LANES)
                near, far = even[:, lanes], odd[:, lanes]
                fields[2 * place, row, :] = jnp.where(lower, near, pltpu.roll(far, half, 1))
                fields[2 * place + 1, row, :] = jnp.where(lower, pltpu.roll(near, half, 1), far)
            serve = jnp.where(lower, serve_ref[0, 2 * pair], serve_ref[0, 2 * pair + 1])
            fields[4, row, :] = serve.astype(f32)
        serve = fields[4]
        tile_cell = jnp.where(serve < 0.0, -1.0, serve * float(BLOCK) + fields[0])
        cell_row = jnp.floor((tile_cell + 0.5) * (1.0 / lon_tile))
        sub = fields[1]
        sub_row = jnp.floor((sub + 0.5) * (1.0 / SUB))
        fields[0] = tile_cell
        fields[1] = cell_row
        fields[4] = sub_row
        fields[5] = tile_cell - cell_row * float(lon_tile)
        fields[6] = sub - sub_row * float(SUB)

        copies[0].wait()
        flat = jnp.concatenate(
            [top_ref[0], tile_ref[...].reshape(cells, channels), bottom_ref[0]], axis=0
        )
        first = jnp.where(lat_pos == 0, 0.0, 1.0)
        last = jnp.where(lat_pos == lax.axis_size("lat") - 1, 0.0, 1.0)
        ends = cells + lon_tile

        def keep(slot, values):
            windows[slot, :lon_tile, :] = (values[:lon_tile] * first).astype(bf16)
            windows[slot, lon_tile:ends, :] = values[lon_tile:ends].astype(bf16)
            windows[slot, ends:, :] = (values[ends:] * last).astype(bf16)

        flat = flat.astype(f32)
        total_rows = flat.shape[0]
        keep(1, flat)
        left = left_ref[...].astype(f32)
        right = right_ref[...].astype(f32)
        shifted[...] = pltpu.roll(flat, 1, 0)
        for row in range(lat_tile + 2):
            shifted[row * lon_tile : row * lon_tile + 1, :] = left[row : row + 1]
        keep(0, shifted[...])
        shifted[...] = pltpu.roll(flat, total_rows - 1, 0)
        for row in range(1, lat_tile + 3):
            shifted[row * lon_tile - 1 : row * lon_tile, :] = right[row - 1 : row]
        keep(2, shifted[...])
        for tap in range(taps):
            top = tap // 3 * lon_tile
            turned[tap] = windows[tap % 3, top : top + cells, :].T
        copies[2].wait()
        features = jnp.zeros((cells, channels), f32)
        for tap in range(taps):
            top = tap // 3 * lon_tile
            features = features + jnp.dot(
                windows[tap % 3, top : top + cells, :], conv_ref[tap], preferred_element_type=f32
            )
        feat_t[...] = features.T.astype(bf16)

        for copy in copies[3:]:
            copy.wait()
        stack0[...] = jnp.zeros_like(stack0)
        if not single:
            sums[...] = jnp.zeros_like(sums)
            later_sums[...] = jnp.zeros_like(later_sums)
        out_sums[...] = jnp.zeros_like(out_sums)

    ids = lax.broadcasted_iota(jnp.int32, (cells, LANES), 0)
    strips = block // LANES
    for strip in range(strips):
        row = pl.ds(step * strips + strip, 1)
        lanes = slice(strip * LANES, (strip + 1) * LANES)
        cell = fields[0, row, :].astype(jnp.int32)
        lefts[:cells, lanes] = jnp.where(ids == cell, 1.0, 0.0).astype(bf16)
        one = jnp.ones((1, LANES), f32)
        group = jnp.concatenate(
            [
                fields[1, row, :],
                fields[4, row, :],
                fields[5, row, :],
                fields[6, row, :],
                fields[2, row, :],
                one,
                jnp.zeros((2, LANES), f32),
            ],
            axis=0,
        )
        coords = jnp.concatenate([group, group, group, jnp.zeros_like(group)], axis=0).astype(
            bf16
        )
        stack0[channels : channels + COORD_ROWS, lanes] = coords
        lefts[cells:left_rows, lanes] = coords[:EXTRA]
    across = (((1,), (1,)), ((), ()))
    spans = block // SPAN
    acts = left_rows + hidden

    def span(index):
        return slice(index * SPAN, (index + 1) * SPAN)

    def first_dots(index):
        lanes = span(index)
        queried = jnp.dot(feat_t[...], lefts[:cells, lanes], preferred_element_type=f32)
        queried = queried.astype(bf16)
        stack0[:channels, lanes] = queried
        lefts[acts:, lanes] = queried
        pre0[:, lanes] = jnp.dot(weight0[...], stack0[:, lanes], preferred_element_type=f32)

    def first_sines(index):
        for top in range(0, hidden, CHUNK):
            for left in range(index * SPAN, (index + 1) * SPAN, LANES):
                at = (slice(top, top + CHUNK), slice(left, left + LANES))
                sine, cosine = sin_cos(pre0[at])
                lefts[left_rows + top : left_rows + top + CHUNK, at[1]] = sine.astype(bf16)
                cos0[at] = cosine

    def second_dots(index):
        lanes = span(index)
        pre1[:, lanes] = jnp.dot(
            weight1[...], lefts[left_rows:, lanes], preferred_element_type=f32
        )

    def second_sines(index):
        for top in range(0, hidden, CHUNK):
            rows = slice(top, top + CHUNK)
            bias = column_tiles[rows, :LANES]
            out_weight = column_tiles[rows, LANES:]
            total = out_sums[rows, :]
            for left in range(index * SPAN, (index + 1) * SPAN, LANES):
                at = (rows, slice(left, left + LANES))
                cotan = fields[3, pl.ds(step * strips + left // LANES, 1), :]
                sine, cosine = sin_cos(pre1[at] + bias)
                total = total + sine * cotan
                rounded1[at] = (out_weight * cotan * cosine).astype(bf16)
            out_sums[rows, :] = total

    def third_dots(index):
        lanes = span(index)
        act_grad = jnp.dot(hidden_ref[...], rounded1[:, lanes], preferred_element_type=f32)
        rounded0[:, lanes] = (act_grad * cos0[:, lanes]).astype(bf16)

    def joins(lanes):
        later = lax.dot_general(
            lefts[:acts, lanes], rounded1[:, lanes], across, preferred_element_type=f32
        )
        early = lax.dot_general(
            lefts[:left_rows, lanes], rounded0[:, lanes], across, preferred_element_type=f32
        )
        if single:
            later_sums[...] = later
            sums[...] = early
        else:
            later_sums[...] += later
            sums[...] += early

    first_dots(0)
    for turn in range(spans + 2):
        if turn + 1 < spans:
            first_dots(turn + 1)
        if turn < spans:
            first_sines(turn)
            second_dots(turn)
        if 0 <= turn - 1 < spans:
            second_sines(turn - 1)
            third_dots(turn - 1)
    joins(slice(0, block))

    @pl.when(step == pl.num_programs(0) - 1)
    def _():
        cell_sums = jnp.concatenate([sums[:cells, :], later_sums[:cells, :]], axis=1)
        upper = cell_sums.astype(bf16)
        lower = (cell_sums - upper.astype(f32)).astype(bf16)
        map_grad = (
            jnp.dot(feat_t[...], upper, preferred_element_type=f32)
            + jnp.dot(feat_t[...], lower, preferred_element_type=f32)
        ) * scale
        feature_grad = (
            lax.dot_general(upper, map_ref[...], across, preferred_element_type=f32)
            + lax.dot_general(lower, map_ref[...], across, preferred_element_type=f32)
        ).astype(bf16)
        feature_grad_ref[...] = feature_grad
        hidden_grad = later_sums[left_rows:, :] * scale
        extra = sums[cells : cells + 8, :]
        later_bias = later_sums[cells + 5 : cells + 6, :]
        total = extra[5:6, :]
        lat_grad = (
            lat_cell * extra[0:1, :] + lat_sub * extra[1:2, :] + lat_offset * total
        )
        lon_grad = (
            lon_cell * extra[2:3, :] + lon_sub * extra[3:4, :] + lon_offset * total
        )
        level_grad = level_cut * extra[4:5, :] + level_offset * total
        out_grad = jnp.sum(out_sums[...].T, axis=0, keepdims=True)
        gain = OMEGA * scale
        small = jnp.concatenate(
            [
                jnp.concatenate([total, later_bias], axis=1) * scale,
                jnp.concatenate([lat_grad, lon_grad], axis=1) * gain,
                jnp.concatenate([level_grad * gain, out_grad * scale], axis=1),
                jnp.zeros((EXTRA - 3, 2 * hidden), f32),
            ],
            axis=0,
        )
        folds = hidden // LANES

        def share(part):
            lanes = slice(part * LANES, (part + 1) * LANES)
            top = part // folds * channels
            left = part % folds * LANES
            return (
                map_grad[:, lanes],
                hidden_grad[top : top + channels, left : left + LANES],
                small[:, lanes],
            )

        half = PARTS // 2
        places = (
            slice(0, channels),
            slice(channels, 2 * channels),
            slice(2 * channels, 2 * channels + EXTRA),
        )
        for part in range(half):
            for place, low, high in zip(places, share(part), share(part + half)):
                kept_ref[part, place, :] = jnp.where(bit == 0, low, high).astype(bf16)
                away_ref[part, place, :] = jnp.where(bit == 0, high, low).astype(bf16)

        rows = taps * channels // PARTS
        for tap in range(taps):
            grad = jnp.dot(turned[tap], feature_grad, preferred_element_type=f32)
            grad = (grad * scale).astype(bf16)
            start = tap * channels
            while start < (tap + 1) * channels:
                end = min((start // rows + 1) * rows, (tap + 1) * channels)
                inside = slice(start % rows, start % rows + end - start)
                value = grad[start - tap * channels : end - tap * channels]
                part = start // rows

                @pl.when(bit == part // half)
                def _():
                    conv_kept_ref[part % half, inside, :] = value

                @pl.when(bit != part // half)
                def _():
                    conv_away_ref[part % half, inside, :] = value

                start = end


def query_pass(
    serve_block,
    got,
    latents,
    rims,
    conv_weight,
    map_weight,
    hidden_weight,
    weights,
    cuts,
    scale,
):
    lat_tile, lon_tile, channels = latents.shape
    cells = lat_tile * lon_tile
    taps = conv_weight.shape[0]
    slots = got.shape[0]
    queries = slots * got.shape[2] // 4
    hidden = hidden_weight.shape[0]
    block = min(TILE, queries)
    f32, bf16 = jnp.float32, jnp.bfloat16
    hbm = pl.BlockSpec(memory_space=pltpu.HBM)
    vmem = pl.BlockSpec(memory_space=pltpu.VMEM)
    share = (PARTS // 2, 2 * channels + EXTRA, LANES)
    conv_share = (PARTS // 2, taps * channels // PARTS, channels)

    return pl.pallas_call(
        functools.partial(query_kernel, cuts, scale, taps, queries == block),
        grid=(queries // block,),
        in_specs=[hbm, vmem, hbm] + [vmem] * 4 + [hbm] * 6,
        out_specs=[vmem] * 5,
        out_shape=[
            jax.ShapeDtypeStruct(share, bf16),
            jax.ShapeDtypeStruct(share, bf16),
            jax.ShapeDtypeStruct(conv_share, bf16),
            jax.ShapeDtypeStruct(conv_share, bf16),
            jax.ShapeDtypeStruct((cells, channels), bf16),
        ],
        scratch_shapes=[
            pltpu.SMEM(serve_block.shape, jnp.int32),
            pltpu.VMEM(latents.shape, bf16),
            pltpu.VMEM(conv_weight.shape, bf16),
            pltpu.VMEM(map_weight.shape, bf16),
            pltpu.VMEM(hidden_weight.shape, bf16),
            *[pltpu.VMEM(value.shape, value.dtype) for value in weights],
            pltpu.SemaphoreType.DMA((8,)),
            pltpu.VMEM((3, cells + 2 * lon_tile, channels), bf16),
            pltpu.VMEM((taps, channels, cells), bf16),
            pltpu.VMEM((cells + 2 * lon_tile, channels), f32),
            pltpu.VMEM((7, slots // 2, LANES), f32),
            pltpu.VMEM((channels, cells), bf16),
            pltpu.VMEM((channels + LANES, block), bf16),
            pltpu.VMEM((cells + EXTRA + hidden + channels, block), bf16),
            pltpu.VMEM((hidden, block), f32),
            pltpu.VMEM((hidden, block), f32),
            pltpu.VMEM((hidden, block), f32),
            pltpu.VMEM((hidden, block), bf16),
            pltpu.VMEM((hidden, block), bf16),
            pltpu.VMEM((cells + EXTRA, hidden), f32),
            pltpu.VMEM((cells + EXTRA + hidden, hidden), f32),
            pltpu.VMEM((hidden, LANES), f32),
        ],
        compiler_params=pltpu.CompilerParams(vmem_limit_bytes=56 * 1000 * 1000),
        name="queries",
    )(
        serve_block,
        got,
        latents,
        *rims,
        conv_weight,
        map_weight,
        hidden_weight,
        *weights,
    )


def bits_of(axis):
    return lax.axis_size(axis).bit_length() - 1


def flip(values, step):
    axis, bit = step
    count = lax.axis_size(axis)
    return lax.ppermute(values, axis, [(i, i ^ (1 << bit)) for i in range(count)])


def own_bit(step):
    axis, bit = step
    return (lax.axis_index(axis) >> bit) & 1


def added(left, right):
    return (left.astype(jnp.float32) + right.astype(jnp.float32)).astype(left.dtype)


def half_sum(kept, got, step, other):
    def pick(values):
        halves = values.reshape((2, values.shape[0] // 2) + values.shape[1:])
        mine = own_bit(step)
        place = 1 - mine if other else mine
        return lax.dynamic_index_in_dim(halves, place, 0, keepdims=False)

    return added(pick(kept), pick(got))


def ring(axis, turn):
    count = lax.axis_size(axis)
    return [(i, (i + turn) % count) for i in range(count)]


def lat_rims(first_row, last_row):
    top = lax.ppermute(last_row, "lat", ring("lat", 1))
    bottom = lax.ppermute(first_row, "lat", ring("lat", -1))
    return top, bottom


def lon_rims(first_col, last_col, top, bottom):
    last = jnp.concatenate([top[:, -1], last_col, bottom[:, -1]], axis=0)
    first = jnp.concatenate([top[:, 0], first_col, bottom[:, 0]], axis=0)
    left = lax.ppermute(last, "lon", ring("lon", 1))
    right = lax.ppermute(first, "lon", ring("lon", -1))
    return left, right


def unpack_kernel(
    mine_a,
    theirs_a,
    mine_b,
    theirs_b,
    conv_ref,
    map_ref,
    bias_ref,
    input_ref,
    hidden_ref,
    out_ref,
):
    f32 = jnp.float32
    channels = map_ref.shape[0]
    folds = hidden_ref.shape[1] // LANES
    half = PARTS // 2
    lon_pos = lax.axis_index("lon")
    bit, bit_first, bit_second = lon_pos & 1, (lon_pos >> 1) & 1, (lon_pos >> 2) & 1

    def place(part, upper_bit, lower_bit):
        upper = 1 - upper_bit if part // 2 % 2 else upper_bit
        lower = 1 - lower_bit if part % 2 else lower_bit
        return upper * 2 + lower

    def fill(low_a, high_a, low_b, high_b):
        for part in range(PARTS):
            source = (low_a if part < half else high_a).at[place(part, bit_first, bit_second)]
            lanes = slice(part * LANES, (part + 1) * LANES)
            top = part // folds * channels
            left = part % folds * LANES
            map_ref[:, lanes] = source[:channels, :].astype(f32)
            hidden_ref[top : top + channels, left : left + LANES] = source[
                channels : 2 * channels, :
            ].astype(f32)
            small = source[2 * channels :, :].astype(f32)
            bias_ref[lanes] = small[0, :]
            side = slice(left, left + LANES)
            input_ref[part // folds, side] = small[1, :]
            if part < folds:
                input_ref[2, side] = small[2, :]
            else:
                out_ref[side] = small[2, :]
            source = (low_b if part < half else high_b).at[place(part, bit_second, bit_first)]
            rows = source.shape[0]
            conv_ref[part * rows : (part + 1) * rows, :] = source[...].astype(f32)

    @pl.when(bit == 0)
    def _():
        fill(mine_a, theirs_a, mine_b, theirs_b)

    @pl.when(bit == 1)
    def _():
        fill(theirs_a, mine_a, theirs_b, mine_b)


def unpacked(pair_a, pair_b, channels, hidden, width, conv_rows):
    f32 = jnp.float32
    vmem = pl.BlockSpec(memory_space=pltpu.VMEM)
    return pl.pallas_call(
        unpack_kernel,
        in_specs=[vmem] * 4,
        out_specs=[vmem] * 6,
        out_shape=[
            jax.ShapeDtypeStruct((conv_rows, channels), f32),
            jax.ShapeDtypeStruct((channels, width), f32),
            jax.ShapeDtypeStruct((width,), f32),
            jax.ShapeDtypeStruct((3, hidden), f32),
            jax.ShapeDtypeStruct((hidden, hidden), f32),
            jax.ShapeDtypeStruct((hidden,), f32),
        ],
        compiler_params=pltpu.CompilerParams(vmem_limit_bytes=20 * 1024 * 1024),
        name="unpack",
    )(*pair_a, *pair_b)


def on_device(
    latents,
    conv_weight,
    map_weight,
    map_bias,
    input_weight,
    hidden_weight,
    output_weight,
    hit_owner,
    serve_block,
    query_grid,
    cotangent,
):
    lat_tile, lon_tile, channels = latents.shape
    lat_parts = lax.axis_size("lat")
    lon_parts = lax.axis_size("lon")
    dev_count = lat_parts * lon_parts
    lat_cells = lat_tile * lat_parts
    lon_cells = lon_tile * lon_parts
    lat_pos = lax.axis_index("lat")
    hit_count = hit_owner.shape[0]
    group_size = cotangent.shape[0] // hit_count
    width = input_weight.shape[1]
    steps = [(axis, bit) for axis in ("lon", "lat") for bit in range(bits_of(axis))]
    core, first, second = steps[:3]
    rest = steps[3:]
    cuts = (
        2.0 / lat_cells,
        2.0 / (lat_cells * SUB),
        2.0 / lon_cells,
        2.0 / (lon_cells * SUB),
        2.0 / LEVELS,
        1.0 / LEVELS - 1.0,
    )
    grad_scale = float(hit_count * group_size * dev_count) ** (-0.5)
    sent, first_row, last_row, first_col, last_col = packed(
        hit_owner, query_grid, cotangent, latents, dev_count, group_size
    )
    sent, late_map = lax.optimization_barrier((sent, map_weight))
    got = lax.all_to_all(sent, ("lat", "lon"), split_axis=0, concat_axis=0, tiled=True)
    top, bottom = lat_rims(first_row, last_row)
    rims = (top, bottom, *lon_rims(first_col, last_col, top, bottom))
    weights = prepared_weights(
        (lat_tile, lon_tile),
        late_map,
        map_bias,
        input_weight,
        hidden_weight[0],
        output_weight,
        cuts,
    )
    kept_a, away_a, kept_b, away_b, feature_grad = query_pass(
        serve_block,
        got,
        latents,
        rims,
        conv_weight,
        map_weight,
        hidden_weight[0],
        weights,
        cuts,
        grad_scale,
    )
    taps = conv_weight.shape[0]
    feature_grad = feature_grad.reshape(lat_tile, lon_tile, channels)
    hold = lax.optimization_barrier
    got_a, got_b = flip(away_a, core), flip(away_b, core)

    away_a, away_b = half_sum(kept_a, got_a, first, 1), half_sum(kept_b, got_b, second, 1)
    away_a, away_b, feature_grad = hold((away_a, away_b, feature_grad))
    kept_a, kept_b = half_sum(kept_a, got_a, first, 0), half_sum(kept_b, got_b, second, 0)
    got_a, got_b = flip(away_a, first), flip(away_b, second)
    top, bottom = lat_rims(feature_grad[:1], feature_grad[-1:])

    away_a, away_b = half_sum(kept_a, got_a, second, 1), half_sum(kept_b, got_b, first, 1)
    away_a, away_b = hold((away_a, away_b))
    kept_a, kept_b = half_sum(kept_a, got_a, second, 0), half_sum(kept_b, got_b, first, 0)
    got_a, got_b = flip(away_a, second), flip(away_b, first)

    sum_a, sum_b = added(kept_a, got_a), added(kept_b, got_b)
    for step_a, step_b in zip(rest, rest[::-1]):
        sum_a, sum_b, top, bottom = hold((sum_a, sum_b, top, bottom))
        got_a = flip(sum_a, step_a)
        got_b = flip(sum_b, step_b)
        if step_a == rest[0]:
            left, right = lon_rims(feature_grad[:, 0], feature_grad[:, -1], top, bottom)
        sum_a, sum_b = added(sum_a, got_a), added(sum_b, got_b)

    for step_a, step_b in ((second, first), (first, second)):
        sum_a, sum_b = hold((sum_a, sum_b))
        got_a = flip(sum_a, step_a)
        got_b = flip(sum_b, step_b)
        sum_a = jnp.concatenate([sum_a, got_a], axis=0)
        sum_b = jnp.concatenate([sum_b, got_b], axis=0)
    sum_a, sum_b = hold((sum_a, sum_b))
    got_a, got_b = flip(sum_a, core), flip(sum_b, core)

    padded_grad = close_poles(
        jnp.concatenate(
            [
                left[:, None],
                jnp.concatenate([top, feature_grad, bottom], axis=0),
                right[:, None],
            ],
            axis=1,
        ),
        lat_pos,
        lat_parts,
    )
    latent_grad = conv_apply(padded_grad, conv_weight, lat_tile, lon_tile, True).reshape(
        lat_tile, lon_tile, channels
    )
    totals = unpacked(
        (sum_a, got_a),
        (sum_b, got_b),
        channels,
        width,
        2 * width,
        taps * channels,
    )
    return (
        latent_grad,
        totals[0].reshape(taps, channels, channels),
        *totals[1:4],
        totals[4][None],
        totals[5],
    )


def solution(mesh):
    placed = (
        P("lat", "lon", None),
        P(),
        P(),
        P(),
        P(),
        P(),
        P(),
        P(("lat", "lon")),
        P(("lat", "lon"), None),
        P(None, ("lat", "lon")),
        P(("lat", "lon")),
    )
    return jax.shard_map(
        on_device,
        mesh=mesh,
        in_specs=placed,
        out_specs=(P("lat", "lon", None), P(), P(), P(), P(), P(), P()),
        check_vma=False,
    )
```

profile of v0, /device:TPU:0, one launch (start us, length us, event | category | flops | bytes accessed | tf_op | source)
XLA Modules:
  0.0 101.7 jit_solution(14558575554325123643)
XLA Ops:
  0.7 1.7 %pack.1 = (f32[32,1,256]{2,1,0:T(1,128)}, bf16[1,16,256]{2,1,0:T(8,128)(2,1)}, bf16[1,16,256]{2,1,0:T(8,128)(2,1)}, bf16[16,256]{1,0:T(8,128)(2,1)}, bf16[16,256]{1,0:T(8,128)(2,1)}) custom-call(s32[24]{0:T(128)} %owner_ref.1, s32[3,1536]{1,0:T(4,128)} %grid_ref.1, f32[1536]{0:T(1024)} %cotan_ref.1, bf16[16,16,256]{2,1,0:T(8,128)(2,1)} %tile_hbm.1), custom_call_target="tpu_custom_call" | custom-call | tf_op jit(solution)/shard_map/pack/pallas_call | solution.py:132
  2.4 3.1 %collective-permute-start = (bf16[1,16,256]{2,1,0:T(8,128)(2,1)}, bf16[1,16,256]{2,1,0:T(8,128)(2,1)S(1)}, u32[]{:S(2)}, u32[]{:S(2)}) collective-permute-start(bf16[1,16,256]{2,1,0:T(8,128)(2,1)} %get-tuple-element.49), channel_id=1, source_target_pairs={{0,8},{8,16},{16,24},{24,0},{1,9},{9,17},{17,25},{25,1},{2,10},{10... | collective-permute-start | bytes 24584 | tf_op jit(solution)/shard_map/ppermute | solution.py:682
  5.4 2.1 %collective-permute-start.1 = (bf16[1,16,256]{2,1,0:T(8,128)(2,1)}, bf16[1,16,256]{2,1,0:T(8,128)(2,1)S(1)}, u32[]{:S(2)}, u32[]{:S(2)}) collective-permute-start(bf16[1,16,256]{2,1,0:T(8,128)(2,1)} %get-tuple-element.50), channel_id=1, source_target_pairs={{0,24},{8,0},{16,8},{24,16},{1,25},{9,1},{17,9},{25,17},{2,26},{10... | collective-permute-start | bytes 24584 | tf_op jit(solution)/shard_map/ppermute | solution.py:683
  7.5 4.2 %all-to-all-start = ((f32[32,1,256]{2,1,0:T(1,128)}), f32[32,1,256]{2,1,0:T(1,128)S(1)}, u32[]{:S(2)}, u32[]{:S(2)}) async-start(f32[32,1,256]{2,1,0:T(1,128)} %get-tuple-element.48), calls=%async_computation | async-start | bytes 65536 | tf_op jit(solution)/shard_map/all_to_all | solution.py:809
  12.5 2.4 %collective-permute-start.3 = (bf16[18,256]{1,0:T(8,128)(2,1)S(1)}, bf16[18,256]{1,0:T(8,128)(2,1)S(1)}, u32[]{:S(2)}, u32[]{:S(2)}) collective-permute-start(bf16[18,256]{1,0:T(8,128)(2,1)S(1)} %pad_maximum_fusion.10), channel_id=1, source_target_pairs={{0,7},{1,0},{2,1},{3,2},{4,3},{5,4},{6,5},{7,6},{8,15},{9,8},{10,9... | collective-permute-start | bytes 27656 | tf_op jit(solution)/shard_map/ppermute | solution.py:691
  15.6 2.7 %weights.1 = (bf16[512,384]{1,0:T(8,128)(2,1)}, bf16[512,768]{1,0:T(8,128)(2,1)}, f32[512,256]{1,0:T(8,128)}) custom-call(bf16[256,1024]{1,0:T(8,128)(2,1)} %map_hbm.1, f32[1024]{0:T(1024)} %refs_1_.1, f32[3,512]{1,0:T(4,128)} %refs_2_.1, bf16[512,512]{1,0:T(8,128)(2,1)} %bitcast.95, f32[512]{0:T(512)} %refs_4_.1), custom_call_target="tpu_custom_call" | custom-call | tf_op jit(solution)/shard_map/weights/pallas_call | solution.py:222
  18.3 1.3 %collective-permute-done.2.left_ref = bf16[18,256]{1,0:T(8,128)(2,1)S(1)} collective-permute-done((bf16[18,256]{1,0:T(8,128)(2,1)S(1)}, bf16[18,256]{1,0:T(8,128)(2,1)S(1)}, u32[]{:S(2)}, u32[]{:S(2)}) %collective-permute-start.2) | collective-permute-done | bytes 9248 | tf_op jit(solution)/shard_map/ppermute | solution.py:690
  19.6 20.0 %queries.1 = (bf16[4,528,128]{2,1,0:T(8,128)(2,1)}, bf16[4,528,128]{2,1,0:T(8,128)(2,1)}, bf16[4,288,256]{2,1,0:T(8,128)(2,1)}, bf16[4,288,256]{2,1,0:T(8,128)(2,1)}, bf16[256,256]{1,0:T(8,128)(2,1)S(1)}) custom-call(s32[1,32]{1,0:T(1,128)S(1)} %copy-done.1, f32[32,1,256]{2,1,0:T(1,128)S(1)} %all-to-all-done.got_ref, bf16[16,16,256]{2,1,0:T(8,128)(2,1)S(1)} %copy-done, ...), custom_call_target="tpu_custom_call" | custom-call | tf_op jit(solution)/shard_map/queries/pallas_call | solution.py:597
  40.2 1.6 %collective-permute-done.4 = bf16[4,528,128]{2,1,0:T(8,128)(2,1)S(1)} collective-permute-done((bf16[4,528,128]{2,1,0:T(8,128)(2,1)}, bf16[4,528,128]{2,1,0:T(8,128)(2,1)S(1)}, u32[]{:S(2)}, u32[]{:S(2)}) %collective-permute-start.4) | collective-permute-done | bytes 540704 | tf_op jit(solution)/shard_map/ppermute | solution.py:654
  41.8 1.2 %add_convert_fusion.3 = (bf16[1,2,528,128]{3,2,1,0:T(8,128)(2,1)S(1)}, bf16[2,528,128]{2,1,0:T(8,128)(2,1)S(1)}) fusion(bf16[2,2,528,128]{3,2,1,0:T(8,128)(2,1)S(1)} %bitcast.100, s32[]{:T(128)S(6)} %select_n.42, bf16[2,2,528,128]{3,2,1,0:T(8,128)(2,1)} %bitcast.99, s32[]{:T(128)S(6)} %select_n.44), kind=kLoop, calls=%fused_computation.13 | loop fusion | flops 1081344 | bytes 1622024 | tf_op jit(solution)/shard_map/convert_element_type | solution.py:663
  43.8 1.5 %collective-permute-start.7 = (bf16[2,288,256]{2,1,0:T(8,128)(2,1)S(1)}, bf16[2,288,256]{2,1,0:T(8,128)(2,1)S(1)}, u32[]{:S(2)}, u32[]{:S(2)}) collective-permute-start(bf16[2,288,256]{2,1,0:T(8,128)(2,1)S(1)} %get-tuple-element.63), channel_id=1, source_target_pairs={{0,4},{1,5},{2,6},{3,7},{4,0},{5,1},{6,2},{7,3},{8,12},{9,13},{10,... | collective-permute-start | bytes 884744 | tf_op jit(solution)/shard_map/ppermute | solution.py:654
  45.3 1.5 %collective-permute-start.10 = (bf16[1,16,256]{2,1,0:T(8,128)(2,1)S(1)}, bf16[1,16,256]{2,1,0:T(8,128)(2,1)S(1)}, u32[]{:S(2)}, u32[]{:S(2)}) collective-permute-start(bf16[1,16,256]{2,1,0:T(8,128)(2,1)S(1)} %get-tuple-element.107), channel_id=1, source_target_pairs={{0,8},{8,16},{16,24},{24,0},{1,9},{9,17},{17,25},{25,1},{2,10},{10... | collective-permute-start | bytes 24584 | tf_op jit(solution)/shard_map/ppermute | solution.py:682
  46.8 2.4 %collective-permute-start.11 = (bf16[1,16,256]{2,1,0:T(8,128)(2,1)S(1)}, bf16[1,16,256]{2,1,0:T(8,128)(2,1)S(1)}, u32[]{:S(2)}, u32[]{:S(2)}) collective-permute-start(bf16[1,16,256]{2,1,0:T(8,128)(2,1)S(1)} %get-tuple-element.106), channel_id=1, source_target_pairs={{0,24},{8,0},{16,8},{24,16},{1,25},{9,1},{17,9},{25,17},{2,26},{10... | collective-permute-start | bytes 24584 | tf_op jit(solution)/shard_map/ppermute | solution.py:683
  49.2 2.6 %collective-permute-done.6 = bf16[2,528,128]{2,1,0:T(8,128)(2,1)S(1)} collective-permute-done((bf16[2,528,128]{2,1,0:T(8,128)(2,1)S(1)}, bf16[2,528,128]{2,1,0:T(8,128)(2,1)S(1)}, u32[]{:S(2)}, u32[]{:S(2)}) %collective-permute-start.6) | collective-permute-done | bytes 270368 | tf_op jit(solution)/shard_map/ppermute | solution.py:654
  51.8 1.0 collective-permute-done.7
  52.9 1.5 %collective-permute-start.8 = (bf16[1,528,128]{2,1,0:T(8,128)(2,1)S(1)}, bf16[1,528,128]{2,1,0:T(8,128)(2,1)S(1)}, u32[]{:S(2)}, u32[]{:S(2)}) collective-permute-start(bf16[1,528,128]{2,1,0:T(8,128)(2,1)S(1)} %fusion.4), channel_id=1, source_target_pairs={{0,4},{1,5},{2,6},{3,7},{4,0},{5,1},{6,2},{7,3},{8,12},{9,13},{10,... | collective-permute-start | bytes 405512 | tf_op jit(solution)/shard_map/ppermute | solution.py:654
  54.7 3.2 %collective-permute-done.8 = bf16[1,528,128]{2,1,0:T(8,128)(2,1)S(1)} collective-permute-done((bf16[1,528,128]{2,1,0:T(8,128)(2,1)S(1)}, bf16[1,528,128]{2,1,0:T(8,128)(2,1)S(1)}, u32[]{:S(2)}, u32[]{:S(2)}) %collective-permute-start.8) | collective-permute-done | bytes 135200 | tf_op jit(solution)/shard_map/ppermute | solution.py:654
  58.0 1.5 %collective-permute-done.9 = bf16[1,288,256]{2,1,0:T(8,128)(2,1)S(1)} collective-permute-done((bf16[1,288,256]{2,1,0:T(8,128)(2,1)S(1)}, bf16[1,288,256]{2,1,0:T(8,128)(2,1)S(1)}, u32[]{:S(2)}, u32[]{:S(2)}) %collective-permute-start.9) | collective-permute-done | bytes 147488 | tf_op jit(solution)/shard_map/ppermute | solution.py:654
  59.6 1.5 %collective-permute-start.13 = (bf16[1,528,128]{2,1,0:T(8,128)(2,1)S(1)}, bf16[1,528,128]{2,1,0:T(8,128)(2,1)S(1)}, u32[]{:S(2)}, u32[]{:S(2)}) collective-permute-start(bf16[1,528,128]{2,1,0:T(8,128)(2,1)S(1)} %add_convert_fusion.9), channel_id=1, source_target_pairs={{0,8},{8,0},{16,24},{24,16},{1,9},{9,1},{17,25},{25,17},{2,10},{10... | collective-permute-start | bytes 405512 | tf_op jit(solution)/shard_map/ppermute | solution.py:654
  61.3 2.7 %collective-permute-start.15 = (bf16[18,256]{1,0:T(8,128)(2,1)S(1)}, bf16[18,256]{1,0:T(8,128)(2,1)S(1)}, u32[]{:S(2)}, u32[]{:S(2)}) collective-permute-start(bf16[18,256]{1,0:T(8,128)(2,1)S(1)} %pad_maximum_fusion.12), channel_id=1, source_target_pairs={{0,7},{1,0},{2,1},{3,2},{4,3},{5,4},{6,5},{7,6},{8,15},{9,8},{10,9... | collective-permute-start | bytes 27656 | tf_op jit(solution)/shard_map/ppermute | solution.py:691
  63.9 2.5 %collective-permute-start.14 = (bf16[1,288,256]{2,1,0:T(8,128)(2,1)S(1)}, bf16[1,288,256]{2,1,0:T(8,128)(2,1)S(1)}, u32[]{:S(2)}, u32[]{:S(2)}) collective-permute-start(bf16[1,288,256]{2,1,0:T(8,128)(2,1)S(1)} %add_convert_fusion.6), channel_id=1, source_target_pairs={{0,16},{8,24},{16,0},{24,8},{1,17},{9,25},{17,1},{25,9},{2,18},{10... | collective-permute-start | bytes 442376 | tf_op jit(solution)/shard_map/ppermute | solution.py:654
  66.5 5.1 %collective-permute-done.14 = bf16[1,288,256]{2,1,0:T(8,128)(2,1)S(1)} collective-permute-done((bf16[1,288,256]{2,1,0:T(8,128)(2,1)S(1)}, bf16[1,288,256]{2,1,0:T(8,128)(2,1)S(1)}, u32[]{:S(2)}, u32[]{:S(2)}) %collective-permute-start.14) | collective-permute-done | bytes 147488 | tf_op jit(solution)/shard_map/ppermute | solution.py:654
  71.8 3.0 %collective-permute-start.16 = (bf16[1,528,128]{2,1,0:T(8,128)(2,1)S(1)}, bf16[1,528,128]{2,1,0:T(8,128)(2,1)S(1)}, u32[]{:S(2)}, u32[]{:S(2)}) collective-permute-start(bf16[1,528,128]{2,1,0:T(8,128)(2,1)S(1)} %add_convert_fusion.8), channel_id=1, source_target_pairs={{0,16},{8,24},{16,0},{24,8},{1,17},{9,25},{17,1},{25,9},{2,18},{10... | collective-permute-start | bytes 405512 | tf_op jit(solution)/shard_map/ppermute | solution.py:654
  75.9 4.0 %collective-permute-done.16 = bf16[1,528,128]{2,1,0:T(8,128)(2,1)S(1)} collective-permute-done((bf16[1,528,128]{2,1,0:T(8,128)(2,1)S(1)}, bf16[1,528,128]{2,1,0:T(8,128)(2,1)S(1)}, u32[]{:S(2)}, u32[]{:S(2)}) %collective-permute-start.16) | collective-permute-done | bytes 135200 | tf_op jit(solution)/shard_map/ppermute | solution.py:654
  79.9 3.1 %collective-permute-start.19 = (bf16[1,288,256]{2,1,0:T(8,128)(2,1)S(1)}, bf16[1,288,256]{2,1,0:T(8,128)(2,1)S(1)}, u32[]{:S(2)}, u32[]{:S(2)}) collective-permute-start(bf16[1,288,256]{2,1,0:T(8,128)(2,1)S(1)} %add_convert_fusion.4), channel_id=1, source_target_pairs={{0,2},{1,3},{2,0},{3,1},{4,6},{5,7},{6,4},{7,5},{8,10},{9,11},{10,... | collective-permute-start | bytes 442376 | tf_op jit(solution)/shard_map/ppermute | solution.py:654
  83.0 1.5 %collective-permute-start.18 = (bf16[1,528,128]{2,1,0:T(8,128)(2,1)S(1)}, bf16[1,528,128]{2,1,0:T(8,128)(2,1)S(1)}, u32[]{:S(2)}, u32[]{:S(2)}) collective-permute-start(bf16[1,528,128]{2,1,0:T(8,128)(2,1)S(1)} %add_convert_fusion.7), channel_id=1, source_target_pairs={{0,4},{1,5},{2,6},{3,7},{4,0},{5,1},{6,2},{7,3},{8,12},{9,13},{10,... | collective-permute-start | bytes 405512 | tf_op jit(solution)/shard_map/ppermute | solution.py:654
  84.7 4.1 %collective-permute-done.18 = bf16[1,528,128]{2,1,0:T(8,128)(2,1)S(1)} collective-permute-done((bf16[1,528,128]{2,1,0:T(8,128)(2,1)S(1)}, bf16[1,528,128]{2,1,0:T(8,128)(2,1)S(1)}, u32[]{:S(2)}, u32[]{:S(2)}) %collective-permute-start.18) | collective-permute-done | bytes 135200 | tf_op jit(solution)/shard_map/ppermute | solution.py:654
  89.4 1.5 %collective-permute-start.21 = (bf16[2,288,256]{2,1,0:T(8,128)(2,1)S(1)}, bf16[2,288,256]{2,1,0:T(8,128)(2,1)S(1)}, u32[]{:S(2)}, u32[]{:S(2)}) collective-permute-start(bf16[2,288,256]{2,1,0:T(8,128)(2,1)S(1)} %pad_maximum_fusion.2), channel_id=1, source_target_pairs={{0,4},{1,5},{2,6},{3,7},{4,0},{5,1},{6,2},{7,3},{8,12},{9,13},{10,... | collective-permute-start | bytes 884744 | tf_op jit(solution)/shard_map/ppermute | solution.py:654
  91.1 4.3 %collective-permute-done.20 = bf16[2,528,128]{2,1,0:T(8,128)(2,1)S(1)} collective-permute-done((bf16[2,528,128]{2,1,0:T(8,128)(2,1)S(1)}, bf16[2,528,128]{2,1,0:T(8,128)(2,1)S(1)}, u32[]{:S(2)}, u32[]{:S(2)}) %collective-permute-start.20) | collective-permute-done | bytes 270368 | tf_op jit(solution)/shard_map/ppermute | solution.py:654
  97.3 0.9 convolution_add_fusion
  98.3 0.9 collective-permute-done.22.theirs_a
  99.1 2.5 %unpack.1 = (f32[2304,256]{1,0:T(8,128)}, f32[256,1024]{1,0:T(8,128)}, f32[1024]{0:T(1024)}, f32[3,512]{1,0:T(4,128)}, f32[512,512]{1,0:T(8,128)}, /*index=5*/f32[512]{0:T(512)}) custom-call(bf16[4,528,128]{2,1,0:T(8,128)(2,1)S(1)} %pad_maximum_fusion.1.mine_a, bf16[4,528,128]{2,1,0:T(8,128)(2,1)S(1)} %collective-permute-done.22.theirs_a, ...), custom_call_target="tpu_custom_call" | custom-call | tf_op jit(solution)/shard_map/unpack/pallas_call | solution.py:753
  (73 shorter events, 7.6 us)
Async XLA Ops:
  0.6 19.0 %copy-start = (bf16[16,16,256]{2,1,0:T(8,128)(2,1)S(1)}, bf16[16,16,256]{2,1,0:T(8,128)(2,1)}, u32[]{:S(2)}) copy-start(bf16[16,16,256]{2,1,0:T(8,128)(2,1)} %tile_hbm.1) | copy-start | bytes 393220
  0.6 19.0 %copy-start.1 = (s32[1,32]{1,0:T(1,128)S(1)}, s32[1,32]{1,0:T(1,128)}, u32[]{:S(2)}) copy-start(s32[1,32]{1,0:T(1,128)} %serve_hbm.1) | copy-start | bytes 388
  2.4 9.4 %collective-permute-start = (bf16[1,16,256]{2,1,0:T(8,128)(2,1)}, bf16[1,16,256]{2,1,0:T(8,128)(2,1)S(1)}, u32[]{:S(2)}, u32[]{:S(2)}) collective-permute-start(bf16[1,16,256]{2,1,0:T(8,128)(2,1)} %get-tuple-element.49), channel_id=1, source_target_pairs={{0,8},{8,16},{16,24},{24,0},{1,9},{9,17},{17,25},{25,1},{2,10},{10... | collective-permute-start | bytes 24584 | tf_op jit(solution)/shard_map/ppermute | solution.py:682
  5.4 6.3 %collective-permute-start.1 = (bf16[1,16,256]{2,1,0:T(8,128)(2,1)}, bf16[1,16,256]{2,1,0:T(8,128)(2,1)S(1)}, u32[]{:S(2)}, u32[]{:S(2)}) collective-permute-start(bf16[1,16,256]{2,1,0:T(8,128)(2,1)} %get-tuple-element.50), channel_id=1, source_target_pairs={{0,24},{8,0},{16,8},{24,16},{1,25},{9,1},{17,9},{25,17},{2,26},{10... | collective-permute-start | bytes 24584 | tf_op jit(solution)/shard_map/ppermute | solution.py:683
  7.5 12.1 %all-to-all-start = ((f32[32,1,256]{2,1,0:T(1,128)}), f32[32,1,256]{2,1,0:T(1,128)S(1)}, u32[]{:S(2)}, u32[]{:S(2)}) async-start(f32[32,1,256]{2,1,0:T(1,128)} %get-tuple-element.48), calls=%async_computation | async-start | bytes 65536 | tf_op jit(solution)/shard_map/all_to_all | solution.py:809
  12.5 5.8 %collective-permute-start.3 = (bf16[18,256]{1,0:T(8,128)(2,1)S(1)}, bf16[18,256]{1,0:T(8,128)(2,1)S(1)}, u32[]{:S(2)}, u32[]{:S(2)}) collective-permute-start(bf16[18,256]{1,0:T(8,128)(2,1)S(1)} %pad_maximum_fusion.10), channel_id=1, source_target_pairs={{0,7},{1,0},{2,1},{3,2},{4,3},{5,4},{6,5},{7,6},{8,15},{9,8},{10,9... | collective-permute-start | bytes 27656 | tf_op jit(solution)/shard_map/ppermute | solution.py:691
  15.6 4.0 %collective-permute-start.2 = (bf16[18,256]{1,0:T(8,128)(2,1)S(1)}, bf16[18,256]{1,0:T(8,128)(2,1)S(1)}, u32[]{:S(2)}, u32[]{:S(2)}) collective-permute-start(bf16[18,256]{1,0:T(8,128)(2,1)S(1)} %pad_maximum_fusion.9), channel_id=1, source_target_pairs={{0,1},{1,2},{2,3},{3,4},{4,5},{5,6},{6,7},{7,0},{8,9},{9,10},{10,1... | collective-permute-start | bytes 27656 | tf_op jit(solution)/shard_map/ppermute | solution.py:690
  39.6 3.4 %copy-start.3 = (bf16[4,288,256]{2,1,0:T(8,128)(2,1)S(1)}, bf16[4,288,256]{2,1,0:T(8,128)(2,1)}, u32[]{:S(2)}) copy-start(bf16[4,288,256]{2,1,0:T(8,128)(2,1)} %get-tuple-element.59) | copy-start | bytes 1769476
  39.6 2.2 %collective-permute-start.4 = (bf16[4,528,128]{2,1,0:T(8,128)(2,1)}, bf16[4,528,128]{2,1,0:T(8,128)(2,1)S(1)}, u32[]{:S(2)}, u32[]{:S(2)}) collective-permute-start(bf16[4,528,128]{2,1,0:T(8,128)(2,1)} %get-tuple-element.58), channel_id=1, source_target_pairs={{0,1},{1,0},{2,3},{3,2},{4,5},{5,4},{6,7},{7,6},{8,9},{9,8},{10,11... | collective-permute-start | bytes 1622024 | tf_op jit(solution)/shard_map/ppermute | solution.py:654
  39.7 3.3 %collective-permute-start.5 = (bf16[4,288,256]{2,1,0:T(8,128)(2,1)}, bf16[4,288,256]{2,1,0:T(8,128)(2,1)S(1)}, u32[]{:S(2)}, u32[]{:S(2)}) collective-permute-start(bf16[4,288,256]{2,1,0:T(8,128)(2,1)} %get-tuple-element.60), channel_id=1, source_target_pairs={{0,1},{1,0},{2,3},{3,2},{4,5},{5,4},{6,7},{7,6},{8,9},{9,8},{10,11... | collective-permute-start | bytes 1769480 | tf_op jit(solution)/shard_map/ppermute | solution.py:654
  43.2 8.6 %collective-permute-start.6 = (bf16[2,528,128]{2,1,0:T(8,128)(2,1)S(1)}, bf16[2,528,128]{2,1,0:T(8,128)(2,1)S(1)}, u32[]{:S(2)}, u32[]{:S(2)}) collective-permute-start(bf16[2,528,128]{2,1,0:T(8,128)(2,1)S(1)} %get-tuple-element.62), channel_id=1, source_target_pairs={{0,2},{1,3},{2,0},{3,1},{4,6},{5,7},{6,4},{7,5},{8,10},{9,11},{10,... | collective-permute-start | bytes 811016 | tf_op jit(solution)/shard_map/ppermute | solution.py:654
  43.8 9.0 %collective-permute-start.7 = (bf16[2,288,256]{2,1,0:T(8,128)(2,1)S(1)}, bf16[2,288,256]{2,1,0:T(8,128)(2,1)S(1)}, u32[]{:S(2)}, u32[]{:S(2)}) collective-permute-start(bf16[2,288,256]{2,1,0:T(8,128)(2,1)S(1)} %get-tuple-element.63), channel_id=1, source_target_pairs={{0,4},{1,5},{2,6},{3,7},{4,0},{5,1},{6,2},{7,3},{8,12},{9,13},{10,... | collective-permute-start | bytes 884744 | tf_op jit(solution)/shard_map/ppermute | solution.py:654
  45.3 14.3 %collective-permute-start.10 = (bf16[1,16,256]{2,1,0:T(8,128)(2,1)S(1)}, bf16[1,16,256]{2,1,0:T(8,128)(2,1)S(1)}, u32[]{:S(2)}, u32[]{:S(2)}) collective-permute-start(bf16[1,16,256]{2,1,0:T(8,128)(2,1)S(1)} %get-tuple-element.107), channel_id=1, source_target_pairs={{0,8},{8,16},{16,24},{24,0},{1,9},{9,17},{17,25},{25,1},{2,10},{10... | collective-permute-start | bytes 24584 | tf_op jit(solution)/shard_map/ppermute | solution.py:682
  46.8 12.8 %collective-permute-start.11 = (bf16[1,16,256]{2,1,0:T(8,128)(2,1)S(1)}, bf16[1,16,256]{2,1,0:T(8,128)(2,1)S(1)}, u32[]{:S(2)}, u32[]{:S(2)}) collective-permute-start(bf16[1,16,256]{2,1,0:T(8,128)(2,1)S(1)} %get-tuple-element.106), channel_id=1, source_target_pairs={{0,24},{8,0},{16,8},{24,16},{1,25},{9,1},{17,9},{25,17},{2,26},{10... | collective-permute-start | bytes 24584 | tf_op jit(solution)/shard_map/ppermute | solution.py:683
  52.9 5.1 %collective-permute-start.8 = (bf16[1,528,128]{2,1,0:T(8,128)(2,1)S(1)}, bf16[1,528,128]{2,1,0:T(8,128)(2,1)S(1)}, u32[]{:S(2)}, u32[]{:S(2)}) collective-permute-start(bf16[1,528,128]{2,1,0:T(8,128)(2,1)S(1)} %fusion.4), channel_id=1, source_target_pairs={{0,4},{1,5},{2,6},{3,7},{4,0},{5,1},{6,2},{7,3},{8,12},{9,13},{10,... | collective-permute-start | bytes 405512 | tf_op jit(solution)/shard_map/ppermute | solution.py:654
  54.4 5.1 %collective-permute-start.9 = (bf16[1,288,256]{2,1,0:T(8,128)(2,1)S(1)}, bf16[1,288,256]{2,1,0:T(8,128)(2,1)S(1)}, u32[]{:S(2)}, u32[]{:S(2)}) collective-permute-start(bf16[1,288,256]{2,1,0:T(8,128)(2,1)S(1)} %fusion.2), channel_id=1, source_target_pairs={{0,2},{1,3},{2,0},{3,1},{4,6},{5,7},{6,4},{7,5},{8,10},{9,11},{10,... | collective-permute-start | bytes 442376 | tf_op jit(solution)/shard_map/ppermute | solution.py:654
  59.6 6.8 %collective-permute-start.13 = (bf16[1,528,128]{2,1,0:T(8,128)(2,1)S(1)}, bf16[1,528,128]{2,1,0:T(8,128)(2,1)S(1)}, u32[]{:S(2)}, u32[]{:S(2)}) collective-permute-start(bf16[1,528,128]{2,1,0:T(8,128)(2,1)S(1)} %add_convert_fusion.9), channel_id=1, source_target_pairs={{0,8},{8,0},{16,24},{24,16},{1,9},{9,1},{17,25},{25,17},{2,10},{10... | collective-permute-start | bytes 405512 | tf_op jit(solution)/shard_map/ppermute | solution.py:654
  61.2 5.2 %collective-permute-start.12 = (bf16[18,256]{1,0:T(8,128)(2,1)S(1)}, bf16[18,256]{1,0:T(8,128)(2,1)S(1)}, u32[]{:S(2)}, u32[]{:S(2)}) collective-permute-start(bf16[18,256]{1,0:T(8,128)(2,1)S(1)} %pad_maximum_fusion.11), channel_id=1, source_target_pairs={{0,1},{1,2},{2,3},{3,4},{4,5},{5,6},{6,7},{7,0},{8,9},{9,10},{10,1... | collective-permute-start | bytes 27656 | tf_op jit(solution)/shard_map/ppermute | solution.py:690
  61.3 5.2 %collective-permute-start.15 = (bf16[18,256]{1,0:T(8,128)(2,1)S(1)}, bf16[18,256]{1,0:T(8,128)(2,1)S(1)}, u32[]{:S(2)}, u32[]{:S(2)}) collective-permute-start(bf16[18,256]{1,0:T(8,128)(2,1)S(1)} %pad_maximum_fusion.12), channel_id=1, source_target_pairs={{0,7},{1,0},{2,1},{3,2},{4,3},{5,4},{6,5},{7,6},{8,15},{9,8},{10,9... | collective-permute-start | bytes 27656 | tf_op jit(solution)/shard_map/ppermute | solution.py:691
  63.9 7.7 %collective-permute-start.14 = (bf16[1,288,256]{2,1,0:T(8,128)(2,1)S(1)}, bf16[1,288,256]{2,1,0:T(8,128)(2,1)S(1)}, u32[]{:S(2)}, u32[]{:S(2)}) collective-permute-start(bf16[1,288,256]{2,1,0:T(8,128)(2,1)S(1)} %add_convert_fusion.6), channel_id=1, source_target_pairs={{0,16},{8,24},{16,0},{24,8},{1,17},{9,25},{17,1},{25,9},{2,18},{10... | collective-permute-start | bytes 442376 | tf_op jit(solution)/shard_map/ppermute | solution.py:654
  71.7 3.4 %copy-start.2 = (bf16[9,256,256]{2,1,0:T(8,128)(2,1)S(1)}, bf16[9,256,256]{2,1,0:T(8,128)(2,1)}, u32[]{:S(2)}) copy-start(bf16[9,256,256]{2,1,0:T(8,128)(2,1)} %conv_hbm.1) | copy-start | bytes 3538948
  71.7 8.2 %collective-permute-start.17 = (bf16[1,288,256]{2,1,0:T(8,128)(2,1)S(1)}, bf16[1,288,256]{2,1,0:T(8,128)(2,1)S(1)}, u32[]{:S(2)}, u32[]{:S(2)}) collective-permute-start(bf16[1,288,256]{2,1,0:T(8,128)(2,1)S(1)} %add_convert_fusion.5), channel_id=1, source_target_pairs={{0,8},{8,0},{16,24},{24,16},{1,9},{9,1},{17,25},{25,17},{2,10},{10... | collective-permute-start | bytes 442376 | tf_op jit(solution)/shard_map/ppermute | solution.py:654
  71.8 8.0 %collective-permute-start.16 = (bf16[1,528,128]{2,1,0:T(8,128)(2,1)S(1)}, bf16[1,528,128]{2,1,0:T(8,128)(2,1)S(1)}, u32[]{:S(2)}, u32[]{:S(2)}) collective-permute-start(bf16[1,528,128]{2,1,0:T(8,128)(2,1)S(1)} %add_convert_fusion.8), channel_id=1, source_target_pairs={{0,16},{8,24},{16,0},{24,8},{1,17},{9,25},{17,1},{25,9},{2,18},{10... | collective-permute-start | bytes 405512 | tf_op jit(solution)/shard_map/ppermute | solution.py:654
  79.9 9.0 %collective-permute-start.19 = (bf16[1,288,256]{2,1,0:T(8,128)(2,1)S(1)}, bf16[1,288,256]{2,1,0:T(8,128)(2,1)S(1)}, u32[]{:S(2)}, u32[]{:S(2)}) collective-permute-start(bf16[1,288,256]{2,1,0:T(8,128)(2,1)S(1)} %add_convert_fusion.4), channel_id=1, source_target_pairs={{0,2},{1,3},{2,0},{3,1},{4,6},{5,7},{6,4},{7,5},{8,10},{9,11},{10,... | collective-permute-start | bytes 442376 | tf_op jit(solution)/shard_map/ppermute | solution.py:654
  83.0 5.8 %collective-permute-start.18 = (bf16[1,528,128]{2,1,0:T(8,128)(2,1)S(1)}, bf16[1,528,128]{2,1,0:T(8,128)(2,1)S(1)}, u32[]{:S(2)}, u32[]{:S(2)}) collective-permute-start(bf16[1,528,128]{2,1,0:T(8,128)(2,1)S(1)} %add_convert_fusion.7), channel_id=1, source_target_pairs={{0,4},{1,5},{2,6},{3,7},{4,0},{5,1},{6,2},{7,3},{8,12},{9,13},{10,... | collective-permute-start | bytes 405512 | tf_op jit(solution)/shard_map/ppermute | solution.py:654
  88.9 6.5 %collective-permute-start.20 = (bf16[2,528,128]{2,1,0:T(8,128)(2,1)S(1)}, bf16[2,528,128]{2,1,0:T(8,128)(2,1)S(1)}, u32[]{:S(2)}, u32[]{:S(2)}) collective-permute-start(bf16[2,528,128]{2,1,0:T(8,128)(2,1)S(1)} %pad_maximum_fusion.3), channel_id=1, source_target_pairs={{0,2},{1,3},{2,0},{3,1},{4,6},{5,7},{6,4},{7,5},{8,10},{9,11},{10,... | collective-permute-start | bytes 811016 | tf_op jit(solution)/shard_map/ppermute | solution.py:654
  89.4 6.8 %collective-permute-start.21 = (bf16[2,288,256]{2,1,0:T(8,128)(2,1)S(1)}, bf16[2,288,256]{2,1,0:T(8,128)(2,1)S(1)}, u32[]{:S(2)}, u32[]{:S(2)}) collective-permute-start(bf16[2,288,256]{2,1,0:T(8,128)(2,1)S(1)} %pad_maximum_fusion.2), channel_id=1, source_target_pairs={{0,4},{1,5},{2,6},{3,7},{4,0},{5,1},{6,2},{7,3},{8,12},{9,13},{10,... | collective-permute-start | bytes 884744 | tf_op jit(solution)/shard_map/ppermute | solution.py:654
  96.3 2.8 %collective-permute-start.23 = (bf16[4,288,256]{2,1,0:T(8,128)(2,1)S(1)}, bf16[4,288,256]{2,1,0:T(8,128)(2,1)S(1)}, u32[]{:S(2)}, u32[]{:S(2)}) collective-permute-start(bf16[4,288,256]{2,1,0:T(8,128)(2,1)S(1)} %pad_maximum_fusion.mine_b), channel_id=1, source_target_pairs={{0,1},{1,0},{2,3},{3,2},{4,5},{5,4},{6,7},{7,6},{8,9},{9,8},{10,11... | collective-permute-start | bytes 1769480 | tf_op jit(solution)/shard_map/ppermute | solution.py:654
  96.4 2.8 %collective-permute-start.22 = (bf16[4,528,128]{2,1,0:T(8,128)(2,1)S(1)}, bf16[4,528,128]{2,1,0:T(8,128)(2,1)S(1)}, u32[]{:S(2)}, u32[]{:S(2)}) collective-permute-start(bf16[4,528,128]{2,1,0:T(8,128)(2,1)S(1)} %pad_maximum_fusion.1.mine_a), channel_id=1, source_target_pairs={{0,1},{1,0},{2,3},{3,2},{4,5},{5,4},{6,7},{7,6},{8,9},{9,8},{10,11... | collective-permute-start | bytes 1622024 | tf_op jit(solution)/shard_map/ppermute | solution.py:654
where the time goes:
time: 102 us
  starting transfers between devices  36.8 us (36%)
  waiting for transfers between devices  30.4 us (30%)
  Pallas kernels  27 us (26%)
  other arithmetic  3.61 us (4%)
  matrix products  2.68 us (3%)
  between operations  1.06 us (1%)
    ppermute x16, waiting for transfers between devices, flip(): return lax.ppermute(values, axis, [(i, i ^ 1 << bit) for i in range(count)])  29.1 us
    pallas_call x1, Pallas kernels, query_pass(): pl.pallas_call(functools.partial(query_kernel, cuts, scale, taps, queries...  20 us
    ppermute x16, starting transfers between devices, flip(): return lax.ppermute(values, axis, [(i, i ^ 1 << bit) for i in range(count)])  18.5 us
    ppermute x2, starting transfers between devices, lon_rims(): right = lax.ppermute(first, 'lon', ring('lon', -1))  5.07 us
    ppermute x2, starting transfers between devices, lat_rims(): top = lax.ppermute(last_row, 'lat', ring('lat', 1))  4.57 us
    ppermute x2, starting transfers between devices, lat_rims(): bottom = lax.ppermute(first_row, 'lat', ring('lat', -1))  4.43 us
    all_to_all x1, starting transfers between devices, on_device(): lax.all_to_all(sent, ('lat', 'lon'), split_axis=0, concat_axis=0, tiled=T...  4.22 us
    pallas_call x1, Pallas kernels, prepared_weights(): pl.pallas_call(functools.partial(weights_kernel, cuts, tile_shape), in_sp...  2.72 us
  transfers between devices with their start and end apart: 25, of which 12 were waited for; matrix products, arithmetic and copies ran while one was open for 6% of the time, Pallas kernels for 3%

commit v1 on v0

--- a/solution.py
+++ b/solution.py
@@ -88,9 +88,23 @@
 
 
 def pack_kernel(
-    owner_ref, grid_ref, cotan_ref, tile_ref, sent_ref, first_row, last_row, first_col, last_col
+    cuts,
+    owner_ref,
+    grid_ref,
+    cotan_ref,
+    tile_ref,
+    bias_ref,
+    input_ref,
+    output_ref,
+    sent_ref,
+    first_row,
+    last_row,
+    first_col,
+    last_col,
+    coef_out,
 ):
     lat_tile, lon_tile, channels = tile_ref.shape
+    coef_kernel(cuts, (lat_tile, lon_tile), bias_ref, input_ref, output_ref, coef_out)
     first_row[...] = tile_ref[:1]
     last_row[...] = tile_ref[lat_tile - 1 :]
     cells = tile_ref[...].reshape(lat_tile * lon_tile, channels).astype(jnp.float32)
@@ -124,24 +138,25 @@
         )
 
 
-def packed(hit_owner, query_grid, cotangent, latents, slots, group_size):
+def packed(hit_owner, query_grid, cotangent, latents, params, cuts, slots, group_size):
     lat_tile, lon_tile, channels = latents.shape
     row = jax.ShapeDtypeStruct((1, lon_tile, channels), latents.dtype)
     column = jax.ShapeDtypeStruct((lat_tile, channels), latents.dtype)
     vmem = pl.BlockSpec(memory_space=pltpu.VMEM)
     return pl.pallas_call(
-        pack_kernel,
-        in_specs=[pl.BlockSpec(memory_space=pltpu.SMEM), vmem, vmem, vmem],
-        out_specs=[vmem] * 5,
+        functools.partial(pack_kernel, cuts),
+        in_specs=[pl.BlockSpec(memory_space=pltpu.SMEM)] + [vmem] * 6,
+        out_specs=[vmem] * 6,
         out_shape=[
             jax.ShapeDtypeStruct((slots, 1, 4 * group_size), jnp.float32),
             row,
             row,
             column,
             column,
+            jax.ShapeDtypeStruct((16, params[1].shape[1]), jnp.float32),
         ],
         name="pack",
-    )(hit_owner, query_grid, cotangent, latents)
+    )(hit_owner, query_grid, cotangent, latents, *params)
 
 
 def fetched(sources, targets, sems):
@@ -154,17 +169,10 @@
     return copies
 
 
-def weights_kernel(cuts, tile_shape, *refs):
-    sources, (weight0, weight1, column_tiles), (*targets, sems) = refs[:5], refs[5:8], refs[8:]
-    map_ref, bias_ref, input_ref, hidden_ref, output_ref = targets
-    for copy in fetched(sources, targets, sems):
-        copy.wait()
-    channels = map_ref.shape[0]
-    hidden = hidden_ref.shape[0]
-    f32, bf16 = jnp.float32, jnp.bfloat16
+def coef_kernel(cuts, tile_shape, bias_ref, input_ref, output_ref, coef_out):
+    hidden = input_ref.shape[1]
     lat_cell, lat_sub, lon_cell, lon_sub, level_cut, level_offset = cuts
     lat_offset, lon_offset = tile_offsets(tile_shape, cuts)
-    weight0[:, :channels] = map_ref[:, :hidden].T
     bias = bias_ref[...].reshape(1, 2 * hidden)
     lat_weight = OMEGA * input_ref[0:1, :]
     lon_weight = OMEGA * input_ref[1:2, :]
@@ -189,6 +197,17 @@
         ],
         axis=0,
     )
+    coef_out[...] = jnp.concatenate(
+        [coef, bias[:, hidden:], output_ref[...].reshape(1, hidden)] + [zero] * 6, axis=0
+    )
+
+
+def prepare_weights(map_ref, hidden_ref, coef_ref, weight0, weight1, column_tiles):
+    channels = map_ref.shape[0]
+    hidden = hidden_ref.shape[0]
+    f32, bf16 = jnp.float32, jnp.bfloat16
+    weight0[:, :channels] = map_ref[:, :hidden].T
+    coef = coef_ref[:8]
     high = coef.astype(bf16).astype(f32)
     mid = (coef - high).astype(bf16).astype(f32)
     low = coef - high - mid
@@ -196,10 +215,8 @@
     weight0[:, channels:] = parts.T.astype(bf16)
     weight1[:, :hidden] = hidden_ref[...].T
     weight1[:, hidden:] = map_ref[:, hidden:].T
-    column_tiles[:, :LANES] = jnp.broadcast_to(bias[:, hidden:], (LANES, hidden)).T
-    column_tiles[:, LANES:] = jnp.broadcast_to(
-        output_ref[...].reshape(1, hidden), (LANES, hidden)
-    ).T
+    column_tiles[:, :LANES] = jnp.broadcast_to(coef_ref[8:9], (LANES, hidden)).T
+    column_tiles[:, LANES:] = jnp.broadcast_to(coef_ref[9:10], (LANES, hidden)).T
 
 
 def tile_offsets(tile_shape, cuts):
@@ -210,28 +227,6 @@
         lat_base.astype(jnp.float32) * (0.5 * lat_step) - 1.0,
         lon_base.astype(jnp.float32) * (0.5 * lon_step) - 1.0,
     )
-
-
-def prepared_weights(
-    tile_shape, map_weight, map_bias, input_weight, hidden_weight, output_weight, cuts
-):
-    channels = map_weight.shape[0]
-    hidden = hidden_weight.shape[0]
-    sources = (map_weight, map_bias, input_weight, hidden_weight, output_weight)
-    vmem = pl.BlockSpec(memory_space=pltpu.VMEM)
-    return pl.pallas_call(
-        functools.partial(weights_kernel, cuts, tile_shape),
-        in_specs=[pl.BlockSpec(memory_space=pltpu.HBM)] * 5,
-        out_specs=[vmem] * 3,
-        out_shape=[
-            jax.ShapeDtypeStruct((hidden, channels + LANES), jnp.bfloat16),
-            jax.ShapeDtypeStruct((hidden, hidden + channels), jnp.bfloat16),
-            jax.ShapeDtypeStruct((hidden, 2 * LANES), jnp.float32),
-        ],
-        scratch_shapes=[pltpu.VMEM(value.shape, value.dtype) for value in sources]
-        + [pltpu.SemaphoreType.DMA((5,))],
-        name="weights",
-    )(*sources)
 
 
 def query_kernel(
@@ -249,9 +244,7 @@
     conv_hbm,
     map_hbm,
     hidden_hbm,
-    weight0_hbm,
-    weight1_hbm,
-    columns_hbm,
+    coef_hbm,
     kept_ref,
     away_ref,
     conv_kept_ref,
@@ -262,6 +255,7 @@
     conv_ref,
     map_ref,
     hidden_ref,
+    coef_ref,
     weight0,
     weight1,
     column_tiles,
@@ -300,22 +294,18 @@
             (
                 tile_hbm,
                 serve_hbm,
+                map_hbm,
+                hidden_hbm,
+                coef_hbm,
                 conv_hbm,
-                weight0_hbm,
-                weight1_hbm,
-                columns_hbm,
-                hidden_hbm,
-                map_hbm,
             ),
             (
                 tile_ref,
                 serve_ref,
+                map_ref,
+                hidden_ref,
+                coef_ref,
                 conv_ref,
-                weight0,
-                weight1,
-                column_tiles,
-                hidden_ref,
-                map_ref,
             ),
             sems,
         )
@@ -372,7 +362,17 @@
         for tap in range(taps):
             top = tap // 3 * lon_tile
             turned[tap] = windows[tap % 3, top : top + cells, :].T
-        copies[2].wait()
+        for copy in copies[2:-1]:
+            copy.wait()
+        prepare_weights(
+            map_ref,
+            hidden_ref,
+            coef_ref,
+            weight0,
+            weight1,
+            column_tiles,
+        )
+        copies[-1].wait()
         features = jnp.zeros((cells, channels), f32)
         for tap in range(taps):
             top = tap // 3 * lon_tile
@@ -381,8 +381,6 @@
             )
         feat_t[...] = features.T.astype(bf16)
 
-        for copy in copies[3:]:
-            copy.wait()
         stack0[...] = jnp.zeros_like(stack0)
         if not single:
             sums[...] = jnp.zeros_like(sums)
@@ -597,7 +595,7 @@
     return pl.pallas_call(
         functools.partial(query_kernel, cuts, scale, taps, queries == block),
         grid=(queries // block,),
-        in_specs=[hbm, vmem, hbm] + [vmem] * 4 + [hbm] * 6,
+        in_specs=[hbm, vmem, hbm] + [vmem] * 4 + [hbm] * 4,
         out_specs=[vmem] * 5,
         out_shape=[
             jax.ShapeDtypeStruct(share, bf16),
@@ -613,6 +611,9 @@
             pltpu.VMEM(map_weight.shape, bf16),
             pltpu.VMEM(hidden_weight.shape, bf16),
             *[pltpu.VMEM(value.shape, value.dtype) for value in weights],
+            pltpu.VMEM((hidden, channels + LANES), bf16),
+            pltpu.VMEM((hidden, hidden + channels), bf16),
+            pltpu.VMEM((hidden, 2 * LANES), f32),
             pltpu.SemaphoreType.DMA((8,)),
             pltpu.VMEM((3, cells + 2 * lon_tile, channels), bf16),
             pltpu.VMEM((taps, channels, cells), bf16),
@@ -802,22 +803,19 @@
         1.0 / LEVELS - 1.0,
     )
     grad_scale = float(hit_count * group_size * dev_count) ** (-0.5)
-    sent, first_row, last_row, first_col, last_col = packed(
-        hit_owner, query_grid, cotangent, latents, dev_count, group_size
-    )
-    sent, late_map = lax.optimization_barrier((sent, map_weight))
+    sent, first_row, last_row, first_col, last_col, coefs = packed(
+        hit_owner,
+        query_grid,
+        cotangent,
+        latents,
+        (map_bias, input_weight, output_weight),
+        cuts,
+        dev_count,
+        group_size,
+    )
     got = lax.all_to_all(sent, ("lat", "lon"), split_axis=0, concat_axis=0, tiled=True)
     top, bottom = lat_rims(first_row, last_row)
     rims = (top, bottom, *lon_rims(first_col, last_col, top, bottom))
-    weights = prepared_weights(
-        (lat_tile, lon_tile),
-        late_map,
-        map_bias,
-        input_weight,
-        hidden_weight[0],
-        output_weight,
-        cuts,
-    )
     kept_a, away_a, kept_b, away_b, feature_grad = query_pass(
         serve_block,
         got,
@@ -826,7 +824,7 @@
         conv_weight,
         map_weight,
         hidden_weight[0],
-        weights,
+        (coefs,),
         cuts,
         grad_scale,
     )

time: 102 us -> 104 us (1.020)
  waiting for transfers between devices: 30.4 us -> 35.4 us
  starting transfers between devices: 36.8 us -> 34.1 us
  Pallas kernels: 27 us -> 24.4 us
  local copies, waits for them, and re-layouts: 0.15 us -> 2.46 us
    pallas_call x2 -> x1, Pallas kernels: 4.44 us -> 1.71 us  [packed(): pl.pallas_call(functools.partial(pack_kernel, cuts), in_specs=[pl.BlockSp...]
    ppermute x16, starting transfers between devices: 18.5 us -> 15.8 us  [flip(): return lax.ppermute(values, axis, [(i, i ^ 1 << bit) for i in range(count)])]
    unnamed x10 -> x12, local copies, waits for them, and re-layouts: 0.03 us -> 2.34 us
    ppermute x16, waiting for transfers between devices: 29.1 us -> 31.3 us  [flip(): return lax.ppermute(values, axis, [(i, i ^ 1 << bit) for i in range(count)])]
    ppermute x2, waiting for transfers between devices: 1.28 us -> 3.32 us  [lon_rims(): left = lax.ppermute(last, 'lon', ring('lon', 1))]
  transfers between devices with their start and end apart: 25 -> 25, of which waited for: 12 -> 13; matrix products, arithmetic and copies ran while one was open for 6% -> 6% of each run, Pallas kernels for 3% -> 0%
where the time goes in v1:
time: 104 us
  waiting for transfers between devices  35.4 us (34%)
  starting transfers between devices  34.1 us (33%)
  Pallas kernels  24.4 us (23%)
  other arithmetic  3.61 us (3%)
  matrix products  2.68 us (3%)
  local copies, waits for them, and re-layouts  2.46 us (2%)
  between operations  1.04 us (1%)
    ppermute x16, waiting for transfers between devices, flip(): return lax.ppermute(values, axis, [(i, i ^ 1 << bit) for i in range(count)])  31.3 us
    pallas_call x1, Pallas kernels, query_pass(): pl.pallas_call(functools.partial(query_kernel, cuts, scale, taps, queries...  20.2 us
    ppermute x16, starting transfers between devices, flip(): return lax.ppermute(values, axis, [(i, i ^ 1 << bit) for i in range(count)])  15.8 us
    ppermute x2, starting transfers between devices, lon_rims(): right = lax.ppermute(first, 'lon', ring('lon', -1))  5.07 us
    ppermute x2, starting transfers between devices, lat_rims(): top = lax.ppermute(last_row, 'lat', ring('lat', 1))  4.57 us
    ppermute x2, starting transfers between devices, lat_rims(): bottom = lax.ppermute(first_row, 'lat', ring('lat', -1))  4.45 us
    all_to_all x1, starting transfers between devices, on_device(): lax.all_to_all(sent, ('lat', 'lon'), split_axis=0, concat_axis=0, tiled=T...  4.21 us
    ppermute x2, waiting for transfers between devices, lon_rims(): left = lax.ppermute(last, 'lon', ring('lon', 1))  3.32 us
  transfers between devices with their start and end apart: 25, of which 13 were waited for; matrix products, arithmetic and copies ran while one was open for 6% of the time, Pallas kernels for 0%

profile of v1, /device:TPU:0, one launch (start us, length us, event | category | flops | bytes accessed | tf_op | source)
XLA Modules:
  0.0 103.7 jit_solution(14784143713800089477)
XLA Ops:
  0.6 1.7 %pack.1 = (f32[32,1,256]{2,1,0:T(1,128)}, bf16[1,16,256]{2,1,0:T(8,128)(2,1)}, bf16[1,16,256]{2,1,0:T(8,128)(2,1)}, bf16[16,256]{1,0:T(8,128)(2,1)}, bf16[16,256]{1,0:T(8,128)(2,1)}, /*index=5*/f32[16,512]{1,0:T(8,128)}) custom-call(s32[24]{0:T(128)} %owner_ref.1, s32[3,1536]{1,0:T(4,128)} %grid_ref.1, f32[1536]{0:T(1024)} %cotan_ref.1, ...), custom_call_target="tpu_custom_call" | custom-call | tf_op jit(solution)/shard_map/pack/pallas_call | solution.py:146
  2.3 3.1 %collective-permute-start = (bf16[1,16,256]{2,1,0:T(8,128)(2,1)}, bf16[1,16,256]{2,1,0:T(8,128)(2,1)S(1)}, u32[]{:S(2)}, u32[]{:S(2)}) collective-permute-start(bf16[1,16,256]{2,1,0:T(8,128)(2,1)} %get-tuple-element.44), channel_id=1, source_target_pairs={{0,8},{8,16},{16,24},{24,0},{1,9},{9,17},{17,25},{25,1},{2,10},{10... | collective-permute-start | bytes 24584 | tf_op jit(solution)/shard_map/ppermute | solution.py:683
  5.4 2.1 %collective-permute-start.1 = (bf16[1,16,256]{2,1,0:T(8,128)(2,1)}, bf16[1,16,256]{2,1,0:T(8,128)(2,1)S(1)}, u32[]{:S(2)}, u32[]{:S(2)}) collective-permute-start(bf16[1,16,256]{2,1,0:T(8,128)(2,1)} %get-tuple-element.45), channel_id=1, source_target_pairs={{0,24},{8,0},{16,8},{24,16},{1,25},{9,1},{17,9},{25,17},{2,26},{10... | collective-permute-start | bytes 24584 | tf_op jit(solution)/shard_map/ppermute | solution.py:684
  7.5 4.2 %all-to-all-start = ((f32[32,1,256]{2,1,0:T(1,128)}), f32[32,1,256]{2,1,0:T(1,128)S(1)}, u32[]{:S(2)}, u32[]{:S(2)}) async-start(f32[32,1,256]{2,1,0:T(1,128)} %get-tuple-element.43), calls=%async_computation | async-start | bytes 65536 | tf_op jit(solution)/shard_map/all_to_all | solution.py:816
  11.8 0.7 pad_maximum_fusion.10
  12.5 2.4 %collective-permute-start.3 = (bf16[18,256]{1,0:T(8,128)(2,1)S(1)}, bf16[18,256]{1,0:T(8,128)(2,1)S(1)}, u32[]{:S(2)}, u32[]{:S(2)}) collective-permute-start(bf16[18,256]{1,0:T(8,128)(2,1)S(1)} %pad_maximum_fusion.10), channel_id=1, source_target_pairs={{0,7},{1,0},{2,1},{3,2},{4,3},{5,4},{6,5},{7,6},{8,15},{9,8},{10,9... | collective-permute-start | bytes 27656 | tf_op jit(solution)/shard_map/ppermute | solution.py:692
  16.3 3.3 %collective-permute-done.2.left_ref = bf16[18,256]{1,0:T(8,128)(2,1)S(1)} collective-permute-done((bf16[18,256]{1,0:T(8,128)(2,1)S(1)}, bf16[18,256]{1,0:T(8,128)(2,1)S(1)}, u32[]{:S(2)}, u32[]{:S(2)}) %collective-permute-start.2) | collective-permute-done | bytes 9248 | tf_op jit(solution)/shard_map/ppermute | solution.py:691
  19.6 0.9 copy-done
  20.5 0.8 copy-done.1
  21.9 20.2 %queries.1 = (bf16[4,528,128]{2,1,0:T(8,128)(2,1)}, bf16[4,528,128]{2,1,0:T(8,128)(2,1)}, bf16[4,288,256]{2,1,0:T(8,128)(2,1)}, bf16[4,288,256]{2,1,0:T(8,128)(2,1)}, bf16[256,256]{1,0:T(8,128)(2,1)S(1)}) custom-call(s32[1,32]{1,0:T(1,128)S(1)} %copy-done.2, f32[32,1,256]{2,1,0:T(1,128)S(1)} %all-to-all-done.got_ref, bf16[16,16,256]{2,1,0:T(8,128)(2,1)S(1)} %copy-done, ...), custom_call_target="tpu_custom_call" | custom-call | tf_op jit(solution)/shard_map/queries/pallas_call | solution.py:595
  42.7 1.6 %collective-permute-done.4 = bf16[4,528,128]{2,1,0:T(8,128)(2,1)S(1)} collective-permute-done((bf16[4,528,128]{2,1,0:T(8,128)(2,1)}, bf16[4,528,128]{2,1,0:T(8,128)(2,1)S(1)}, u32[]{:S(2)}, u32[]{:S(2)}) %collective-permute-start.4) | collective-permute-done | bytes 540704 | tf_op jit(solution)/shard_map/ppermute | solution.py:655
  44.3 1.2 %add_convert_fusion.3 = (bf16[1,2,528,128]{3,2,1,0:T(8,128)(2,1)S(1)}, bf16[2,528,128]{2,1,0:T(8,128)(2,1)S(1)}) fusion(bf16[2,2,528,128]{3,2,1,0:T(8,128)(2,1)S(1)} %bitcast.98, s32[]{:T(128)S(6)} %select_n.42, bf16[2,2,528,128]{3,2,1,0:T(8,128)(2,1)} %bitcast.97, s32[]{:T(128)S(6)} %select_n.44), kind=kLoop, calls=%fused_computation.13 | loop fusion | flops 1081344 | bytes 1622024 | tf_op jit(solution)/shard_map/convert_element_type | solution.py:664
  46.4 1.5 %collective-permute-start.10 = (bf16[1,16,256]{2,1,0:T(8,128)(2,1)S(1)}, bf16[1,16,256]{2,1,0:T(8,128)(2,1)S(1)}, u32[]{:S(2)}, u32[]{:S(2)}) collective-permute-start(bf16[1,16,256]{2,1,0:T(8,128)(2,1)S(1)} %get-tuple-element.99), channel_id=1, source_target_pairs={{0,8},{8,16},{16,24},{24,0},{1,9},{9,17},{17,25},{25,1},{2,10},{10... | collective-permute-start | bytes 24584 | tf_op jit(solution)/shard_map/ppermute | solution.py:683
  47.9 2.4 %collective-permute-start.11 = (bf16[1,16,256]{2,1,0:T(8,128)(2,1)S(1)}, bf16[1,16,256]{2,1,0:T(8,128)(2,1)S(1)}, u32[]{:S(2)}, u32[]{:S(2)}) collective-permute-start(bf16[1,16,256]{2,1,0:T(8,128)(2,1)S(1)} %get-tuple-element.98), channel_id=1, source_target_pairs={{0,24},{8,0},{16,8},{24,16},{1,25},{9,1},{17,9},{25,17},{2,26},{10... | collective-permute-start | bytes 24584 | tf_op jit(solution)/shard_map/ppermute | solution.py:684
  50.3 4.0 %collective-permute-done.6 = bf16[2,528,128]{2,1,0:T(8,128)(2,1)S(1)} collective-permute-done((bf16[2,528,128]{2,1,0:T(8,128)(2,1)S(1)}, bf16[2,528,128]{2,1,0:T(8,128)(2,1)S(1)}, u32[]{:S(2)}, u32[]{:S(2)}) %collective-permute-start.6) | collective-permute-done | bytes 270368 | tf_op jit(solution)/shard_map/ppermute | solution.py:655
  55.5 1.7 %collective-permute-start.9 = (bf16[1,288,256]{2,1,0:T(8,128)(2,1)S(1)}, bf16[1,288,256]{2,1,0:T(8,128)(2,1)S(1)}, u32[]{:S(2)}, u32[]{:S(2)}) collective-permute-start(bf16[1,288,256]{2,1,0:T(8,128)(2,1)S(1)} %fusion.2), channel_id=1, source_target_pairs={{0,2},{1,3},{2,0},{3,1},{4,6},{5,7},{6,4},{7,5},{8,10},{9,11},{10,... | collective-permute-start | bytes 442376 | tf_op jit(solution)/shard_map/ppermute | solution.py:655
  57.2 2.8 %collective-permute-done.8 = bf16[1,528,128]{2,1,0:T(8,128)(2,1)S(1)} collective-permute-done((bf16[1,528,128]{2,1,0:T(8,128)(2,1)S(1)}, bf16[1,528,128]{2,1,0:T(8,128)(2,1)S(1)}, u32[]{:S(2)}, u32[]{:S(2)}) %collective-permute-start.8) | collective-permute-done | bytes 135200 | tf_op jit(solution)/shard_map/ppermute | solution.py:655
  60.8 1.5 %collective-permute-start.13 = (bf16[1,528,128]{2,1,0:T(8,128)(2,1)S(1)}, bf16[1,528,128]{2,1,0:T(8,128)(2,1)S(1)}, u32[]{:S(2)}, u32[]{:S(2)}) collective-permute-start(bf16[1,528,128]{2,1,0:T(8,128)(2,1)S(1)} %add_convert_fusion.9), channel_id=1, source_target_pairs={{0,8},{8,0},{16,24},{24,16},{1,9},{9,1},{17,25},{25,17},{2,10},{10... | collective-permute-start | bytes 405512 | tf_op jit(solution)/shard_map/ppermute | solution.py:655
  62.4 2.7 %collective-permute-start.15 = (bf16[18,256]{1,0:T(8,128)(2,1)S(1)}, bf16[18,256]{1,0:T(8,128)(2,1)S(1)}, u32[]{:S(2)}, u32[]{:S(2)}) collective-permute-start(bf16[18,256]{1,0:T(8,128)(2,1)S(1)} %pad_maximum_fusion.12), channel_id=1, source_target_pairs={{0,7},{1,0},{2,1},{3,2},{4,3},{5,4},{6,5},{7,6},{8,15},{9,8},{10,9... | collective-permute-start | bytes 27656 | tf_op jit(solution)/shard_map/ppermute | solution.py:692
  65.1 2.4 %collective-permute-start.14 = (bf16[1,288,256]{2,1,0:T(8,128)(2,1)S(1)}, bf16[1,288,256]{2,1,0:T(8,128)(2,1)S(1)}, u32[]{:S(2)}, u32[]{:S(2)}) collective-permute-start(bf16[1,288,256]{2,1,0:T(8,128)(2,1)S(1)} %add_convert_fusion.6), channel_id=1, source_target_pairs={{0,16},{8,24},{16,0},{24,8},{1,17},{9,25},{17,1},{25,9},{2,18},{10... | collective-permute-start | bytes 442376 | tf_op jit(solution)/shard_map/ppermute | solution.py:655
  67.6 6.5 %collective-permute-done.14 = bf16[1,288,256]{2,1,0:T(8,128)(2,1)S(1)} collective-permute-done((bf16[1,288,256]{2,1,0:T(8,128)(2,1)S(1)}, bf16[1,288,256]{2,1,0:T(8,128)(2,1)S(1)}, u32[]{:S(2)}, u32[]{:S(2)}) %collective-permute-start.14) | collective-permute-done | bytes 147488 | tf_op jit(solution)/shard_map/ppermute | solution.py:655
  74.2 2.9 %collective-permute-start.16 = (bf16[1,528,128]{2,1,0:T(8,128)(2,1)S(1)}, bf16[1,528,128]{2,1,0:T(8,128)(2,1)S(1)}, u32[]{:S(2)}, u32[]{:S(2)}) collective-permute-start(bf16[1,528,128]{2,1,0:T(8,128)(2,1)S(1)} %add_convert_fusion.8), channel_id=1, source_target_pairs={{0,16},{8,24},{16,0},{24,8},{1,17},{9,25},{17,1},{25,9},{2,18},{10... | collective-permute-start | bytes 405512 | tf_op jit(solution)/shard_map/ppermute | solution.py:655
  78.3 5.3 %collective-permute-done.16 = bf16[1,528,128]{2,1,0:T(8,128)(2,1)S(1)} collective-permute-done((bf16[1,528,128]{2,1,0:T(8,128)(2,1)S(1)}, bf16[1,528,128]{2,1,0:T(8,128)(2,1)S(1)}, u32[]{:S(2)}, u32[]{:S(2)}) %collective-permute-start.16) | collective-permute-done | bytes 135200 | tf_op jit(solution)/shard_map/ppermute | solution.py:655
  83.7 1.1 %collective-permute-start.19 = (bf16[1,288,256]{2,1,0:T(8,128)(2,1)S(1)}, bf16[1,288,256]{2,1,0:T(8,128)(2,1)S(1)}, u32[]{:S(2)}, u32[]{:S(2)}) collective-permute-start(bf16[1,288,256]{2,1,0:T(8,128)(2,1)S(1)} %add_convert_fusion.4), channel_id=1, source_target_pairs={{0,2},{1,3},{2,0},{3,1},{4,6},{5,7},{6,4},{7,5},{8,10},{9,11},{10,... | collective-permute-start | bytes 442376 | tf_op jit(solution)/shard_map/ppermute | solution.py:655
  85.5 4.6 %collective-permute-done.18 = bf16[1,528,128]{2,1,0:T(8,128)(2,1)S(1)} collective-permute-done((bf16[1,528,128]{2,1,0:T(8,128)(2,1)S(1)}, bf16[1,528,128]{2,1,0:T(8,128)(2,1)S(1)}, u32[]{:S(2)}, u32[]{:S(2)}) %collective-permute-start.18) | collective-permute-done | bytes 135200 | tf_op jit(solution)/shard_map/ppermute | solution.py:655
  90.2 0.8 collective-permute-start.20
  91.3 2.2 %collective-permute-start.21 = (bf16[2,288,256]{2,1,0:T(8,128)(2,1)S(1)}, bf16[2,288,256]{2,1,0:T(8,128)(2,1)S(1)}, u32[]{:S(2)}, u32[]{:S(2)}) collective-permute-start(bf16[2,288,256]{2,1,0:T(8,128)(2,1)S(1)} %pad_maximum_fusion.2), channel_id=1, source_target_pairs={{0,4},{1,5},{2,6},{3,7},{4,0},{5,1},{6,2},{7,3},{8,12},{9,13},{10,... | collective-permute-start | bytes 884744 | tf_op jit(solution)/shard_map/ppermute | solution.py:655
  93.8 3.0 %collective-permute-done.20 = bf16[2,528,128]{2,1,0:T(8,128)(2,1)S(1)} collective-permute-done((bf16[2,528,128]{2,1,0:T(8,128)(2,1)S(1)}, bf16[2,528,128]{2,1,0:T(8,128)(2,1)S(1)}, u32[]{:S(2)}, u32[]{:S(2)}) %collective-permute-start.20) | collective-permute-done | bytes 270368 | tf_op jit(solution)/shard_map/ppermute | solution.py:655
  96.8 1.4 %collective-permute-done.21 = bf16[2,288,256]{2,1,0:T(8,128)(2,1)S(1)} collective-permute-done((bf16[2,288,256]{2,1,0:T(8,128)(2,1)S(1)}, bf16[2,288,256]{2,1,0:T(8,128)(2,1)S(1)}, u32[]{:S(2)}, u32[]{:S(2)}) %collective-permute-start.21) | collective-permute-done | bytes 294944 | tf_op jit(solution)/shard_map/ppermute | solution.py:655
  99.3 0.9 convolution_add_fusion
  100.3 0.9 collective-permute-done.22.theirs_a
  101.2 2.5 %unpack.1 = (f32[2304,256]{1,0:T(8,128)}, f32[256,1024]{1,0:T(8,128)}, f32[1024]{0:T(1024)}, f32[3,512]{1,0:T(4,128)}, f32[512,512]{1,0:T(8,128)}, /*index=5*/f32[512]{0:T(512)}) custom-call(bf16[4,528,128]{2,1,0:T(8,128)(2,1)S(1)} %pad_maximum_fusion.1.mine_a, bf16[4,528,128]{2,1,0:T(8,128)(2,1)S(1)} %collective-permute-done.22.theirs_a, ...), custom_call_target="tpu_custom_call" | custom-call | tf_op jit(solution)/shard_map/unpack/pallas_call | solution.py:754
  (74 shorter events, 9.2 us)
Async XLA Ops:
  2.3 9.4 %collective-permute-start = (bf16[1,16,256]{2,1,0:T(8,128)(2,1)}, bf16[1,16,256]{2,1,0:T(8,128)(2,1)S(1)}, u32[]{:S(2)}, u32[]{:S(2)}) collective-permute-start(bf16[1,16,256]{2,1,0:T(8,128)(2,1)} %get-tuple-element.44), channel_id=1, source_target_pairs={{0,8},{8,16},{16,24},{24,0},{1,9},{9,17},{17,25},{25,1},{2,10},{10... | collective-permute-start | bytes 24584 | tf_op jit(solution)/shard_map/ppermute | solution.py:683
  5.4 6.3 %collective-permute-start.1 = (bf16[1,16,256]{2,1,0:T(8,128)(2,1)}, bf16[1,16,256]{2,1,0:T(8,128)(2,1)S(1)}, u32[]{:S(2)}, u32[]{:S(2)}) collective-permute-start(bf16[1,16,256]{2,1,0:T(8,128)(2,1)} %get-tuple-element.45), channel_id=1, source_target_pairs={{0,24},{8,0},{16,8},{24,16},{1,25},{9,1},{17,9},{25,17},{2,26},{10... | collective-permute-start | bytes 24584 | tf_op jit(solution)/shard_map/ppermute | solution.py:684
  7.5 12.1 %all-to-all-start = ((f32[32,1,256]{2,1,0:T(1,128)}), f32[32,1,256]{2,1,0:T(1,128)S(1)}, u32[]{:S(2)}, u32[]{:S(2)}) async-start(f32[32,1,256]{2,1,0:T(1,128)} %get-tuple-element.43), calls=%async_computation | async-start | bytes 65536 | tf_op jit(solution)/shard_map/all_to_all | solution.py:816
  12.5 3.8 %collective-permute-start.3 = (bf16[18,256]{1,0:T(8,128)(2,1)S(1)}, bf16[18,256]{1,0:T(8,128)(2,1)S(1)}, u32[]{:S(2)}, u32[]{:S(2)}) collective-permute-start(bf16[18,256]{1,0:T(8,128)(2,1)S(1)} %pad_maximum_fusion.10), channel_id=1, source_target_pairs={{0,7},{1,0},{2,1},{3,2},{4,3},{5,4},{6,5},{7,6},{8,15},{9,8},{10,9... | collective-permute-start | bytes 27656 | tf_op jit(solution)/shard_map/ppermute | solution.py:692
  15.6 4.0 %collective-permute-start.2 = (bf16[18,256]{1,0:T(8,128)(2,1)S(1)}, bf16[18,256]{1,0:T(8,128)(2,1)S(1)}, u32[]{:S(2)}, u32[]{:S(2)}) collective-permute-start(bf16[18,256]{1,0:T(8,128)(2,1)S(1)} %pad_maximum_fusion.9), channel_id=1, source_target_pairs={{0,1},{1,2},{2,3},{3,4},{4,5},{5,6},{6,7},{7,0},{8,9},{9,10},{10,1... | collective-permute-start | bytes 27656 | tf_op jit(solution)/shard_map/ppermute | solution.py:691
  19.6 0.9 copy-start
  20.5 0.8 copy-start.1
  21.2 0.7 copy-start.2
  42.1 3.4 %copy-start.4 = (bf16[4,288,256]{2,1,0:T(8,128)(2,1)S(1)}, bf16[4,288,256]{2,1,0:T(8,128)(2,1)}, u32[]{:S(2)}) copy-start(bf16[4,288,256]{2,1,0:T(8,128)(2,1)} %get-tuple-element.51) | copy-start | bytes 1769476
  42.1 2.2 %collective-permute-start.4 = (bf16[4,528,128]{2,1,0:T(8,128)(2,1)}, bf16[4,528,128]{2,1,0:T(8,128)(2,1)S(1)}, u32[]{:S(2)}, u32[]{:S(2)}) collective-permute-start(bf16[4,528,128]{2,1,0:T(8,128)(2,1)} %get-tuple-element.50), channel_id=1, source_target_pairs={{0,1},{1,0},{2,3},{3,2},{4,5},{5,4},{6,7},{7,6},{8,9},{9,8},{10,11... | collective-permute-start | bytes 1622024 | tf_op jit(solution)/shard_map/ppermute | solution.py:655
  42.2 3.3 %collective-permute-start.5 = (bf16[4,288,256]{2,1,0:T(8,128)(2,1)}, bf16[4,288,256]{2,1,0:T(8,128)(2,1)S(1)}, u32[]{:S(2)}, u32[]{:S(2)}) collective-permute-start(bf16[4,288,256]{2,1,0:T(8,128)(2,1)} %get-tuple-element.52), channel_id=1, source_target_pairs={{0,1},{1,0},{2,3},{3,2},{4,5},{5,4},{6,7},{7,6},{8,9},{9,8},{10,11... | collective-permute-start | bytes 1769480 | tf_op jit(solution)/shard_map/ppermute | solution.py:655
  45.7 8.6 %collective-permute-start.6 = (bf16[2,528,128]{2,1,0:T(8,128)(2,1)S(1)}, bf16[2,528,128]{2,1,0:T(8,128)(2,1)S(1)}, u32[]{:S(2)}, u32[]{:S(2)}) collective-permute-start(bf16[2,528,128]{2,1,0:T(8,128)(2,1)S(1)} %get-tuple-element.54), channel_id=1, source_target_pairs={{0,2},{1,3},{2,0},{3,1},{4,6},{5,7},{6,4},{7,5},{8,10},{9,11},{10,... | collective-permute-start | bytes 811016 | tf_op jit(solution)/shard_map/ppermute | solution.py:655
  45.8 9.1 %collective-permute-start.7 = (bf16[2,288,256]{2,1,0:T(8,128)(2,1)S(1)}, bf16[2,288,256]{2,1,0:T(8,128)(2,1)S(1)}, u32[]{:S(2)}, u32[]{:S(2)}) collective-permute-start(bf16[2,288,256]{2,1,0:T(8,128)(2,1)S(1)} %get-tuple-element.55), channel_id=1, source_target_pairs={{0,4},{1,5},{2,6},{3,7},{4,0},{5,1},{6,2},{7,3},{8,12},{9,13},{10,... | collective-permute-start | bytes 884744 | tf_op jit(solution)/shard_map/ppermute | solution.py:655
  46.4 14.3 %collective-permute-start.10 = (bf16[1,16,256]{2,1,0:T(8,128)(2,1)S(1)}, bf16[1,16,256]{2,1,0:T(8,128)(2,1)S(1)}, u32[]{:S(2)}, u32[]{:S(2)}) collective-permute-start(bf16[1,16,256]{2,1,0:T(8,128)(2,1)S(1)} %get-tuple-element.99), channel_id=1, source_target_pairs={{0,8},{8,16},{16,24},{24,0},{1,9},{9,17},{17,25},{25,1},{2,10},{10... | collective-permute-start | bytes 24584 | tf_op jit(solution)/shard_map/ppermute | solution.py:683
  47.9 12.8 %collective-permute-start.11 = (bf16[1,16,256]{2,1,0:T(8,128)(2,1)S(1)}, bf16[1,16,256]{2,1,0:T(8,128)(2,1)S(1)}, u32[]{:S(2)}, u32[]{:S(2)}) collective-permute-start(bf16[1,16,256]{2,1,0:T(8,128)(2,1)S(1)} %get-tuple-element.98), channel_id=1, source_target_pairs={{0,24},{8,0},{16,8},{24,16},{1,25},{9,1},{17,9},{25,17},{2,26},{10... | collective-permute-start | bytes 24584 | tf_op jit(solution)/shard_map/ppermute | solution.py:684
  54.9 5.1 %collective-permute-start.8 = (bf16[1,528,128]{2,1,0:T(8,128)(2,1)S(1)}, bf16[1,528,128]{2,1,0:T(8,128)(2,1)S(1)}, u32[]{:S(2)}, u32[]{:S(2)}) collective-permute-start(bf16[1,528,128]{2,1,0:T(8,128)(2,1)S(1)} %fusion.4), channel_id=1, source_target_pairs={{0,4},{1,5},{2,6},{3,7},{4,0},{5,1},{6,2},{7,3},{8,12},{9,13},{10,... | collective-permute-start | bytes 405512 | tf_op jit(solution)/shard_map/ppermute | solution.py:655
  55.5 5.1 %collective-permute-start.9 = (bf16[1,288,256]{2,1,0:T(8,128)(2,1)S(1)}, bf16[1,288,256]{2,1,0:T(8,128)(2,1)S(1)}, u32[]{:S(2)}, u32[]{:S(2)}) collective-permute-start(bf16[1,288,256]{2,1,0:T(8,128)(2,1)S(1)} %fusion.2), channel_id=1, source_target_pairs={{0,2},{1,3},{2,0},{3,1},{4,6},{5,7},{6,4},{7,5},{8,10},{9,11},{10,... | collective-permute-start | bytes 442376 | tf_op jit(solution)/shard_map/ppermute | solution.py:655
  60.8 6.8 %collective-permute-start.13 = (bf16[1,528,128]{2,1,0:T(8,128)(2,1)S(1)}, bf16[1,528,128]{2,1,0:T(8,128)(2,1)S(1)}, u32[]{:S(2)}, u32[]{:S(2)}) collective-permute-start(bf16[1,528,128]{2,1,0:T(8,128)(2,1)S(1)} %add_convert_fusion.9), channel_id=1, source_target_pairs={{0,8},{8,0},{16,24},{24,16},{1,9},{9,1},{17,25},{25,17},{2,10},{10... | collective-permute-start | bytes 405512 | tf_op jit(solution)/shard_map/ppermute | solution.py:655
  62.3 5.2 %collective-permute-start.12 = (bf16[18,256]{1,0:T(8,128)(2,1)S(1)}, bf16[18,256]{1,0:T(8,128)(2,1)S(1)}, u32[]{:S(2)}, u32[]{:S(2)}) collective-permute-start(bf16[18,256]{1,0:T(8,128)(2,1)S(1)} %pad_maximum_fusion.11), channel_id=1, source_target_pairs={{0,1},{1,2},{2,3},{3,4},{4,5},{5,6},{6,7},{7,0},{8,9},{9,10},{10,1... | collective-permute-start | bytes 27656 | tf_op jit(solution)/shard_map/ppermute | solution.py:691
  62.4 5.1 %collective-permute-start.15 = (bf16[18,256]{1,0:T(8,128)(2,1)S(1)}, bf16[18,256]{1,0:T(8,128)(2,1)S(1)}, u32[]{:S(2)}, u32[]{:S(2)}) collective-permute-start(bf16[18,256]{1,0:T(8,128)(2,1)S(1)} %pad_maximum_fusion.12), channel_id=1, source_target_pairs={{0,7},{1,0},{2,1},{3,2},{4,3},{5,4},{6,5},{7,6},{8,15},{9,8},{10,9... | collective-permute-start | bytes 27656 | tf_op jit(solution)/shard_map/ppermute | solution.py:692
  65.1 9.0 %collective-permute-start.14 = (bf16[1,288,256]{2,1,0:T(8,128)(2,1)S(1)}, bf16[1,288,256]{2,1,0:T(8,128)(2,1)S(1)}, u32[]{:S(2)}, u32[]{:S(2)}) collective-permute-start(bf16[1,288,256]{2,1,0:T(8,128)(2,1)S(1)} %add_convert_fusion.6), channel_id=1, source_target_pairs={{0,16},{8,24},{16,0},{24,8},{1,17},{9,25},{17,1},{25,9},{2,18},{10... | collective-permute-start | bytes 442376 | tf_op jit(solution)/shard_map/ppermute | solution.py:655
  74.1 3.3 %copy-start.3 = (bf16[9,256,256]{2,1,0:T(8,128)(2,1)S(1)}, bf16[9,256,256]{2,1,0:T(8,128)(2,1)}, u32[]{:S(2)}) copy-start(bf16[9,256,256]{2,1,0:T(8,128)(2,1)} %conv_hbm.1) | copy-start | bytes 3538948
  74.2 9.5 %collective-permute-start.17 = (bf16[1,288,256]{2,1,0:T(8,128)(2,1)S(1)}, bf16[1,288,256]{2,1,0:T(8,128)(2,1)S(1)}, u32[]{:S(2)}, u32[]{:S(2)}) collective-permute-start(bf16[1,288,256]{2,1,0:T(8,128)(2,1)S(1)} %add_convert_fusion.5), channel_id=1, source_target_pairs={{0,8},{8,0},{16,24},{24,16},{1,9},{9,1},{17,25},{25,17},{2,10},{10... | collective-permute-start | bytes 442376 | tf_op jit(solution)/shard_map/ppermute | solution.py:655
  74.2 9.3 %collective-permute-start.16 = (bf16[1,528,128]{2,1,0:T(8,128)(2,1)S(1)}, bf16[1,528,128]{2,1,0:T(8,128)(2,1)S(1)}, u32[]{:S(2)}, u32[]{:S(2)}) collective-permute-start(bf16[1,528,128]{2,1,0:T(8,128)(2,1)S(1)} %add_convert_fusion.8), channel_id=1, source_target_pairs={{0,16},{8,24},{16,0},{24,8},{1,17},{9,25},{17,1},{25,9},{2,18},{10... | collective-permute-start | bytes 405512 | tf_op jit(solution)/shard_map/ppermute | solution.py:655
  83.7 6.5 %collective-permute-start.19 = (bf16[1,288,256]{2,1,0:T(8,128)(2,1)S(1)}, bf16[1,288,256]{2,1,0:T(8,128)(2,1)S(1)}, u32[]{:S(2)}, u32[]{:S(2)}) collective-permute-start(bf16[1,288,256]{2,1,0:T(8,128)(2,1)S(1)} %add_convert_fusion.4), channel_id=1, source_target_pairs={{0,2},{1,3},{2,0},{3,1},{4,6},{5,7},{6,4},{7,5},{8,10},{9,11},{10,... | collective-permute-start | bytes 442376 | tf_op jit(solution)/shard_map/ppermute | solution.py:655
  84.8 5.3 %collective-permute-start.18 = (bf16[1,528,128]{2,1,0:T(8,128)(2,1)S(1)}, bf16[1,528,128]{2,1,0:T(8,128)(2,1)S(1)}, u32[]{:S(2)}, u32[]{:S(2)}) collective-permute-start(bf16[1,528,128]{2,1,0:T(8,128)(2,1)S(1)} %add_convert_fusion.7), channel_id=1, source_target_pairs={{0,4},{1,5},{2,6},{3,7},{4,0},{5,1},{6,2},{7,3},{8,12},{9,13},{10,... | collective-permute-start | bytes 405512 | tf_op jit(solution)/shard_map/ppermute | solution.py:655
  90.2 6.5 %collective-permute-start.20 = (bf16[2,528,128]{2,1,0:T(8,128)(2,1)S(1)}, bf16[2,528,128]{2,1,0:T(8,128)(2,1)S(1)}, u32[]{:S(2)}, u32[]{:S(2)}) collective-permute-start(bf16[2,528,128]{2,1,0:T(8,128)(2,1)S(1)} %pad_maximum_fusion.3), channel_id=1, source_target_pairs={{0,2},{1,3},{2,0},{3,1},{4,6},{5,7},{6,4},{7,5},{8,10},{9,11},{10,... | collective-permute-start | bytes 811016 | tf_op jit(solution)/shard_map/ppermute | solution.py:655
  91.3 6.9 %collective-permute-start.21 = (bf16[2,288,256]{2,1,0:T(8,128)(2,1)S(1)}, bf16[2,288,256]{2,1,0:T(8,128)(2,1)S(1)}, u32[]{:S(2)}, u32[]{:S(2)}) collective-permute-start(bf16[2,288,256]{2,1,0:T(8,128)(2,1)S(1)} %pad_maximum_fusion.2), channel_id=1, source_target_pairs={{0,4},{1,5},{2,6},{3,7},{4,0},{5,1},{6,2},{7,3},{8,12},{9,13},{10,... | collective-permute-start | bytes 884744 | tf_op jit(solution)/shard_map/ppermute | solution.py:655
  98.3 2.8 %collective-permute-start.23 = (bf16[4,288,256]{2,1,0:T(8,128)(2,1)S(1)}, bf16[4,288,256]{2,1,0:T(8,128)(2,1)S(1)}, u32[]{:S(2)}, u32[]{:S(2)}) collective-permute-start(bf16[4,288,256]{2,1,0:T(8,128)(2,1)S(1)} %pad_maximum_fusion.mine_b), channel_id=1, source_target_pairs={{0,1},{1,0},{2,3},{3,2},{4,5},{5,4},{6,7},{7,6},{8,9},{9,8},{10,11... | collective-permute-start | bytes 1769480 | tf_op jit(solution)/shard_map/ppermute | solution.py:655
  98.4 2.8 %collective-permute-start.22 = (bf16[4,528,128]{2,1,0:T(8,128)(2,1)S(1)}, bf16[4,528,128]{2,1,0:T(8,128)(2,1)S(1)}, u32[]{:S(2)}, u32[]{:S(2)}) collective-permute-start(bf16[4,528,128]{2,1,0:T(8,128)(2,1)S(1)} %pad_maximum_fusion.1.mine_a), channel_id=1, source_target_pairs={{0,1},{1,0},{2,3},{3,2},{4,5},{5,4},{6,7},{7,6},{8,9},{9,8},{10,11... | collective-permute-start | bytes 1622024 | tf_op jit(solution)/shard_map/ppermute | solution.py:655
